TPU v7x, 32 devices: a whole 2x2x4 slice. The times are simulated.
32 devices in a mesh: row: 8 (over z, x), col: 4 (over y, core).
Axes of the slice: x: 2, y: 2, z: 4, core: 2. Of those that a mesh axis runs over, the one named last changes fastest.
Arguments:
- coeff: bfloat16 [8192, 512], P('row'), may hold values from -6 to 6
- tri_blocks: bfloat16 [5120, 256, 128], P(('row', 'col')), may hold values from -0.0390625 to 0.0390625
- pair_aux: int32 [5120], P(('row', 'col')), may hold values from 0 to 7
- pair_ao: int32 [5120], P(('row', 'col')), may hold values from 0 to 7
- owner_slot: int32 [4, 8], P('col'), may hold values from 0 to 15, as said below
- metric_blocks: bfloat16 [2048, 128, 128], P(('row', 'col')), may hold values from -0.125 to 0.125
- pair_slot: int32 [2048], P(('row', 'col')), may hold values from 0 to 1
- pair_out: int32 [2048], P(('row', 'col')), may hold values from 0 to 7
Outputs:
- transformed: bfloat16 [8192, 1024], P(('row', 'col'))
Inputs may be any that keep to these rules, and one draw needn't show every extreme that they name: `owner_slot`: within a column the 8 entries are distinct slots; slot s belongs to row s // 2; in every column some row receives 2 blocks.
All inputs are finite; a program needn't handle non-finite values.
Results may differ from a plain program's by a relative error of at most 0.014.
Values may be sent and summed in bfloat16 or wider, within the bound.
No kernel may reach another device: no remote copies, remote signals or barrier semaphores. Data moves between devices by JAX's collectives and lax.ppermute only.
A program may use at most 128 MiB of HBM per device.

v0:
```python
import math

import jax
import jax.numpy as jnp
from jax import lax
from jax.sharding import PartitionSpec as P

BLOCK = 128
OCC = 512
NUW = 2
MAXOWN = 2
QB_DEV = 2


def one_hot_rows(ids, count):
    return ids[:, None] == jnp.arange(count, dtype=jnp.int32)[None, :]


def first_section(tiles, aux_ids, ao_ids, coeff_blocks, segments):
    count = tiles.shape[0]
    group_size = math.gcd(count, 32)
    width = NUW * OCC
    table_size = coeff_blocks.shape[0]
    tile_sets = tiles.reshape(count // group_size, group_size, BLOCK * NUW, BLOCK)
    aux_sets = aux_ids.reshape(count // group_size, group_size)
    ao_sets = ao_ids.reshape(count // group_size, group_size)

    def first_advance(total, pieces):
        tile_set, aux_set, ao_set = pieces
        picker = one_hot_rows(ao_set, table_size).astype(jnp.bfloat16)
        gathered = jnp.einsum(
            "kt,tbo->kbo", picker, coeff_blocks, preferred_element_type=jnp.float32
        ).astype(jnp.bfloat16)
        products = jnp.einsum(
            "kab,kbo->kao", tile_set, gathered, preferred_element_type=jnp.float32
        )
        products = products.reshape(group_size, BLOCK * width)
        sorter = one_hot_rows(aux_set, segments).astype(jnp.float32)
        added = jnp.dot(
            sorter.T, products, precision=lax.Precision.HIGHEST, preferred_element_type=jnp.float32
        )
        return (total + added.reshape(segments, BLOCK, width), None)

    start = jnp.zeros((segments, BLOCK, width), jnp.float32)
    total, unused = lax.scan(first_advance, start, (tile_sets, aux_sets, ao_sets))
    return total


def second_section(metric, slot_ids, out_ids, owned, segments):
    count = metric.shape[0]
    group_size = math.gcd(count, 32)
    width = NUW * OCC
    table_size = owned.shape[0]
    metric_sets = metric.reshape(count // group_size, group_size, BLOCK, BLOCK)
    slot_sets = slot_ids.reshape(count // group_size, group_size)
    out_sets = out_ids.reshape(count // group_size, group_size)

    def second_advance(total, pieces):
        metric_set, slot_set, out_set = pieces
        picker = one_hot_rows(slot_set, table_size).astype(jnp.bfloat16)
        gathered = jnp.einsum(
            "kt,tbw->kbw", picker, owned, preferred_element_type=jnp.float32
        ).astype(jnp.bfloat16)
        products = jnp.einsum(
            "kab,kbw->kaw", metric_set, gathered, preferred_element_type=jnp.float32
        )
        products = products.reshape(group_size, BLOCK * width)
        sorter = one_hot_rows(out_set, segments).astype(jnp.float32)
        added = jnp.dot(
            sorter.T, products, precision=lax.Precision.HIGHEST, preferred_element_type=jnp.float32
        )
        return (total + added.reshape(segments, BLOCK, width), None)

    start = jnp.zeros((segments, BLOCK, width), jnp.float32)
    total, unused = lax.scan(second_advance, start, (metric_sets, slot_sets, out_sets))
    return total


def add_sources(blocks):
    return jnp.sum(blocks, axis=0, dtype=jnp.float32)


def per_device(
    coeff, tri_blocks, pair_aux, pair_ao, owner_slot, metric_blocks, pair_slot, pair_out
):
    row_count = lax.axis_size("row")
    col_count = lax.axis_size("col")
    width = NUW * OCC
    column_blocks = owner_slot.shape[1]
    coeff_blocks = coeff.reshape(-1, BLOCK, OCC)
    partial_value = first_section(tri_blocks, pair_aux, pair_ao, coeff_blocks, column_blocks)
    rounded = partial_value.astype(jnp.bfloat16).reshape(column_blocks, BLOCK * width)
    placer = one_hot_rows(owner_slot[0], row_count * MAXOWN).astype(jnp.bfloat16)
    outgoing = jnp.dot(placer.T, rounded, preferred_element_type=jnp.float32).astype(jnp.bfloat16)
    outgoing = outgoing.reshape(row_count * MAXOWN, BLOCK, width)
    received = add_sources(
        lax.all_to_all(
            outgoing.reshape(row_count, MAXOWN, BLOCK, width),
            "row",
            split_axis=0,
            concat_axis=0,
            tiled=True,
        )
    )
    owned = received.astype(jnp.bfloat16)
    terms = second_section(metric_blocks, pair_slot, pair_out, owned, col_count * QB_DEV)
    summed = lax.psum_scatter(terms.astype(jnp.bfloat16), "col", scatter_dimension=0, tiled=True)
    return summed.reshape(QB_DEV * BLOCK, width)


def solution(mesh):
    in_specs = (
        P("row", None),
        P(("row", "col"), None, None),
        P(("row", "col")),
        P(("row", "col")),
        P("col", None),
        P(("row", "col"), None, None),
        P(("row", "col")),
        P(("row", "col")),
    )
    out_specs = P(("row", "col"), None)
    return jax.shard_map(
        per_device, mesh=mesh, in_specs=in_specs, out_specs=out_specs, check_vma=False
    )
```

profile of v0, /device:TPU:0, one launch (start us, length us, event | category | flops | bytes accessed | tf_op | source)
XLA Modules:
  0.0 419.2 jit_solution(1339715332506632533)
XLA Ops:
  6.5 1.8 copy.28
  8.3 0.8 reshape.49
  9.1 0.8 reshape.51
  9.9 157.4 %while.22 = (s32[]{:T(128)}, f32[8,128,1024]{2,0,1:T(8,128)}, s32[5,32]{1,0:T(8,128)S(1)}, bf16[5,32,256,128]{3,2,1,0:T(8,128)(2,1)}, s32[5,32]{1,0:T(8,128)S(1)...) while((s32[]{:T(128)}, f32[8,128,1024]{2,0,1:T(8,128)}, s32[5,32]{1,0:T(8,128)S(1)}, ...), condition=%wide.region_1.2_spmd.clone, body=%wide.region_0.1_spmd.clone.sunk | while | flops 1514144256 | bytes 87033184 | solution.py:45
  9.9 1.3 convolution_convert_fusion.5
  11.2 7.3 %fusion.64 = f32[32,256,512]{2,1,0:T(8,128)S(1)} fusion(bf16[32,128,512]{2,0,1:T(8,128)(2,1)S(1)} %convolution_convert_fusion.5, bf16[5,32,256,128]{3,2,1,0:T(8,128)(2,1)} %get-tuple-element.260, s32[]{:T(128)} %get-tuple-element.249), kind=kOutput, calls=%fused_computation.3.clone.1 | convolution fusion | flops 1073741824 | bytes 23069184 | tf_op jit(solution)/shard_map/while/body/eval_jaxpr/kab,kbo->kao/dot_general | solution.py:34
  18.5 11.7 %copy.65 = f32[4,8,256,512]{3,1,2,0:T(8,128)} copy(f32[4,8,256,512]{3,2,1,0:T(8,128)S(1)} %bitcast.93) | data formatting | bytes 33554432 | tf_op jit(solution)/shard_map/while
  30.2 10.6 %select_add_fusion.4 = f32[8,128,1024]{2,0,1:T(8,128)} fusion(f32[8,128,1024]{2,0,1:T(8,128)} %get-tuple-element.250, pred[]{:T(512)S(6)} %compare.6, f32[4,128,8,1024]{3,2,1,0:T(8,128)} %bitcast.95, s32[32]{0:T(128)S(1)} %get-tuple-element.232), kind=kOutput, calls=%fused_computation.5.clone.1 | convolution fusion | flops 404750592 | bytes 25165952 | tf_op jit(solution)/shard_map/while/body/eval_jaxpr/dot_general | solution.py:39
  40.8 1.3 convolution_convert_fusion.5
  42.1 7.3 %fusion.64 = f32[32,256,512]{2,1,0:T(8,128)S(1)} fusion(bf16[32,128,512]{2,0,1:T(8,128)(2,1)S(1)} %convolution_convert_fusion.5, bf16[5,32,256,128]{3,2,1,0:T(8,128)(2,1)} %get-tuple-element.260, s32[]{:T(128)} %get-tuple-element.249), kind=kOutput, calls=%fused_computation.3.clone.1 | convolution fusion | flops 1073741824 | bytes 23069184 | tf_op jit(solution)/shard_map/while/body/eval_jaxpr/kab,kbo->kao/dot_general | solution.py:34
  49.4 11.7 %copy.65 = f32[4,8,256,512]{3,1,2,0:T(8,128)} copy(f32[4,8,256,512]{3,2,1,0:T(8,128)S(1)} %bitcast.93) | data formatting | bytes 33554432 | tf_op jit(solution)/shard_map/while
  61.1 11.2 %select_add_fusion.4 = f32[8,128,1024]{2,0,1:T(8,128)} fusion(f32[8,128,1024]{2,0,1:T(8,128)} %get-tuple-element.250, pred[]{:T(512)S(6)} %compare.6, f32[4,128,8,1024]{3,2,1,0:T(8,128)} %bitcast.95, s32[32]{0:T(128)S(1)} %get-tuple-element.232), kind=kOutput, calls=%fused_computation.5.clone.1 | convolution fusion | flops 404750592 | bytes 25165952 | tf_op jit(solution)/shard_map/while/body/eval_jaxpr/dot_general | solution.py:39
  72.3 1.3 convolution_convert_fusion.5
  73.6 7.3 %fusion.64 = f32[32,256,512]{2,1,0:T(8,128)S(1)} fusion(bf16[32,128,512]{2,0,1:T(8,128)(2,1)S(1)} %convolution_convert_fusion.5, bf16[5,32,256,128]{3,2,1,0:T(8,128)(2,1)} %get-tuple-element.260, s32[]{:T(128)} %get-tuple-element.249), kind=kOutput, calls=%fused_computation.3.clone.1 | convolution fusion | flops 1073741824 | bytes 23069184 | tf_op jit(solution)/shard_map/while/body/eval_jaxpr/kab,kbo->kao/dot_general | solution.py:34
  80.9 11.7 %copy.65 = f32[4,8,256,512]{3,1,2,0:T(8,128)} copy(f32[4,8,256,512]{3,2,1,0:T(8,128)S(1)} %bitcast.93) | data formatting | bytes 33554432 | tf_op jit(solution)/shard_map/while
  92.6 11.2 %select_add_fusion.4 = f32[8,128,1024]{2,0,1:T(8,128)} fusion(f32[8,128,1024]{2,0,1:T(8,128)} %get-tuple-element.250, pred[]{:T(512)S(6)} %compare.6, f32[4,128,8,1024]{3,2,1,0:T(8,128)} %bitcast.95, s32[32]{0:T(128)S(1)} %get-tuple-element.232), kind=kOutput, calls=%fused_computation.5.clone.1 | convolution fusion | flops 404750592 | bytes 25165952 | tf_op jit(solution)/shard_map/while/body/eval_jaxpr/dot_general | solution.py:39
  103.9 1.3 convolution_convert_fusion.5
  105.2 7.3 %fusion.64 = f32[32,256,512]{2,1,0:T(8,128)S(1)} fusion(bf16[32,128,512]{2,0,1:T(8,128)(2,1)S(1)} %convolution_convert_fusion.5, bf16[5,32,256,128]{3,2,1,0:T(8,128)(2,1)} %get-tuple-element.260, s32[]{:T(128)} %get-tuple-element.249), kind=kOutput, calls=%fused_computation.3.clone.1 | convolution fusion | flops 1073741824 | bytes 23069184 | tf_op jit(solution)/shard_map/while/body/eval_jaxpr/kab,kbo->kao/dot_general | solution.py:34
  112.5 11.7 %copy.65 = f32[4,8,256,512]{3,1,2,0:T(8,128)} copy(f32[4,8,256,512]{3,2,1,0:T(8,128)S(1)} %bitcast.93) | data formatting | bytes 33554432 | tf_op jit(solution)/shard_map/while
  124.2 11.2 %select_add_fusion.4 = f32[8,128,1024]{2,0,1:T(8,128)} fusion(f32[8,128,1024]{2,0,1:T(8,128)} %get-tuple-element.250, pred[]{:T(512)S(6)} %compare.6, f32[4,128,8,1024]{3,2,1,0:T(8,128)} %bitcast.95, s32[32]{0:T(128)S(1)} %get-tuple-element.232), kind=kOutput, calls=%fused_computation.5.clone.1 | convolution fusion | flops 404750592 | bytes 25165952 | tf_op jit(solution)/shard_map/while/body/eval_jaxpr/dot_general | solution.py:39
  135.4 1.3 convolution_convert_fusion.5
  136.7 7.3 %fusion.64 = f32[32,256,512]{2,1,0:T(8,128)S(1)} fusion(bf16[32,128,512]{2,0,1:T(8,128)(2,1)S(1)} %convolution_convert_fusion.5, bf16[5,32,256,128]{3,2,1,0:T(8,128)(2,1)} %get-tuple-element.260, s32[]{:T(128)} %get-tuple-element.249), kind=kOutput, calls=%fused_computation.3.clone.1 | convolution fusion | flops 1073741824 | bytes 23069184 | tf_op jit(solution)/shard_map/while/body/eval_jaxpr/kab,kbo->kao/dot_general | solution.py:34
  144.0 11.7 %copy.65 = f32[4,8,256,512]{3,1,2,0:T(8,128)} copy(f32[4,8,256,512]{3,2,1,0:T(8,128)S(1)} %bitcast.93) | data formatting | bytes 33554432 | tf_op jit(solution)/shard_map/while
  155.8 11.2 %select_add_fusion.4 = f32[8,128,1024]{2,0,1:T(8,128)} fusion(f32[8,128,1024]{2,0,1:T(8,128)} %get-tuple-element.250, pred[]{:T(512)S(6)} %compare.6, f32[4,128,8,1024]{3,2,1,0:T(8,128)} %bitcast.95, s32[32]{0:T(128)S(1)} %get-tuple-element.232), kind=kOutput, calls=%fused_computation.5.clone.1 | convolution fusion | flops 404750592 | bytes 25165952 | tf_op jit(solution)/shard_map/while/body/eval_jaxpr/dot_general | solution.py:39
  167.2 0.0 copy-start.1
  167.2 2.5 convert_element_type.13
  169.8 0.0 copy-done.1
  169.8 1.7 convolution_convert_fusion.2
  171.4 4.3 %copy.35 = bf16[2,8,128,1024]{3,2,1,0:T(8,128)(2,1)} copy(bf16[2,8,128,1024]{3,1,2,0:T(8,128)(2,1)S(1)} %bitcast.97) | data formatting | bytes 8388608
  175.8 0.0 copy-start.2
  175.8 0.0 copy-start.3
  175.8 7.4 %all-to-all-start = ((bf16[8,2,128,1024]{3,2,1,0:T(8,128)(2,1)}), bf16[8,2,128,1024]{3,2,1,0:T(8,128)(2,1)}, u32[]{:S(2)}, u32[]{:S(2)}) async-start(bf16[8,2,128,1024]{3,2,1,0:T(8,128)(2,1)} %bitcast.96), calls=%async_computation | async-start | bytes 8388608 | tf_op jit(solution)/shard_map/all_to_all | solution.py:97
  183.2 0.0 copy-start
  183.2 0.0 reduce-scatter.2.cloned.1.call-start
  183.2 0.0 copy-done.2
  183.2 0.1 reshape.46
  183.3 0.0 copy-done.3
  183.3 0.1 reshape.48
  183.4 93.0 %all-to-all-done = bf16[8,2,128,1024]{3,2,1,0:T(8,128)(2,1)} async-done(((bf16[8,2,128,1024]{3,2,1,0:T(8,128)(2,1)}), bf16[8,2,128,1024]{3,2,1,0:T(8,128)(2,1)}, u32[]{:S(2)}, u32[]{:S(2)}) %all-to-all-start) | async-done | bytes 4194336 | tf_op jit(solution)/shard_map/all_to_all | solution.py:97
  276.4 3.1 reduce_sum.12
  279.5 0.5 copy.29
  280.1 0.0 copy-done
  280.1 95.5 %while.23 = (s32[]{:T(128)}, f32[8,128,1024]{2,0,1:T(8,128)}, s32[2,32]{1,0:T(2,128)S(1)}, bf16[2,32,128,128]{3,2,1,0:T(8,128)(2,1)S(1)}, s32[2,32]{1,0:T(2,128)...) while((s32[]{:T(128)}, f32[8,128,1024]{2,0,1:T(8,128)}, ...), condition=%wide.region_4.5_spmd.clone, body=%wide.region_3.4_spmd.clone.sunk | while | flops 1499464064 | bytes 60293988 | solution.py:75
  294.0 2.7 convolution_convert_fusion.6
  296.7 16.2 %fusion.72 = f32[32,128,1024]{2,1,0:T(8,128)} fusion(bf16[32,128,1024]{2,0,1:T(8,128)(2,1)S(1)} %convolution_convert_fusion.6, bf16[2,32,128,128]{3,2,1,0:T(8,128)(2,1)S(1)} %get-tuple-element.284, s32[]{:T(128)} %get-tuple-element.273), kind=kOutput, calls=%fused_computation.23.clone.1 | convolution fusion | flops 1073741824 | bytes 26214404 | tf_op jit(solution)/shard_map/while/body/eval_jaxpr/kab,kbw->kaw/dot_general | solution.py:64
  312.9 21.5 %select_add_fusion.5 = f32[8,128,1024]{2,0,1:T(8,128)} fusion(f32[8,128,1024]{2,0,1:T(8,128)} %get-tuple-element.274, pred[]{:T(512)S(6)} %compare.7, s32[32]{0:T(128)S(1)} %get-tuple-element.239, f32[4,8,128,1024]{3,2,1,0:T(8,128)} %bitcast.94), kind=kOutput, calls=%fused_computation.26.clone.1 | convolution fusion | flops 404750592 | bytes 25165952 | tf_op jit(solution)/shard_map/while/body/eval_jaxpr/dot_general | solution.py:69
  334.4 2.7 convolution_convert_fusion.6
  337.1 16.2 %fusion.72 = f32[32,128,1024]{2,1,0:T(8,128)} fusion(bf16[32,128,1024]{2,0,1:T(8,128)(2,1)S(1)} %convolution_convert_fusion.6, bf16[2,32,128,128]{3,2,1,0:T(8,128)(2,1)S(1)} %get-tuple-element.284, s32[]{:T(128)} %get-tuple-element.273), kind=kOutput, calls=%fused_computation.23.clone.1 | convolution fusion | flops 1073741824 | bytes 26214404 | tf_op jit(solution)/shard_map/while/body/eval_jaxpr/kab,kbw->kaw/dot_general | solution.py:64
  353.3 22.1 %select_add_fusion.5 = f32[8,128,1024]{2,0,1:T(8,128)} fusion(f32[8,128,1024]{2,0,1:T(8,128)} %get-tuple-element.274, pred[]{:T(512)S(6)} %compare.7, s32[32]{0:T(128)S(1)} %get-tuple-element.239, f32[4,8,128,1024]{3,2,1,0:T(8,128)} %bitcast.94), kind=kOutput, calls=%fused_computation.26.clone.1 | convolution fusion | flops 404750592 | bytes 25165952 | tf_op jit(solution)/shard_map/while/body/eval_jaxpr/dot_general | solution.py:69
  375.6 5.8 %copy.53 = bf16[8,128,1024]{2,1,0:T(8,128)(2,1)} copy(f32[8,128,1024]{2,0,1:T(8,128)} %get-tuple-element.70) | data formatting | bytes 6291456 | tf_op jit(solution)/shard_map/while | solution.py:75
  381.4 0.0 reduce-scatter.2.cloned.1.call-update
  381.4 30.7 %reduce-scatter.2.cloned.1.call-done = bf16[2,128,1024]{2,1,0:T(8,128)(2,1)} async-done(((bf16[8,128,1024]{2,1,0:T(8,128)(2,1)}), bf16[2,128,1024]{2,1,0:T(8,128)(2,1)}) %reduce-scatter.2.cloned.1.call-update) | async-done | bytes 524304 | tf_op jit(solution)/shard_map/reduce_scatter | solution.py:107
  (9 shorter events, 0.0 us)
Async XLA Ops:
  167.2 2.5 copy-start.1
  175.8 7.5 %copy-start.2 = (s32[64]{0:T(128)S(1)}, s32[64]{0:T(128)}, u32[]{:S(2)}) copy-start(s32[64]{0:T(128)} %param.19) | copy-start | bytes 772
  175.8 7.6 %copy-start.3 = (s32[64]{0:T(128)S(1)}, s32[64]{0:T(128)}, u32[]{:S(2)}) copy-start(s32[64]{0:T(128)} %param.18) | copy-start | bytes 772
  175.8 100.7 %all-to-all-start = ((bf16[8,2,128,1024]{3,2,1,0:T(8,128)(2,1)}), bf16[8,2,128,1024]{3,2,1,0:T(8,128)(2,1)}, u32[]{:S(2)}, u32[]{:S(2)}) async-start(bf16[8,2,128,1024]{3,2,1,0:T(8,128)(2,1)} %bitcast.96), calls=%async_computation | async-start | bytes 8388608 | tf_op jit(solution)/shard_map/all_to_all | solution.py:97
  183.2 96.9 %copy-start = (bf16[64,128,128]{2,1,0:T(8,128)(2,1)S(1)}, bf16[64,128,128]{2,1,0:T(8,128)(2,1)}, u32[]{:S(2)}) copy-start(bf16[64,128,128]{2,1,0:T(8,128)(2,1)} %param.17) | copy-start | bytes 6291460
  183.2 228.9 %reduce-scatter.2.cloned.1.call-start = ((), (), s32[]{:S(2)}) async-start(), calls=%async_computation.2 | async-start | bytes 2621440 | tf_op jit(solution)/shard_map/reduce_scatter | solution.py:107
Sparse Core Ops, SparseCore 0:
  381.5 30.5 reduce-scatter.1
where the time goes:
time: 422 us; the launch traced here: 419 us
  matrix products  182 us (43%)
  waiting for transfers between devices  124 us (29%)
  local copies, waits for them, and re-layouts  72.8 us (17%)
  loops' own time  14.4 us (3%)
  between operations  13.7 us (3%)
  starting transfers between devices  7.44 us (2%)
  other arithmetic  5.62 us (1%)
    all_to_all x1, waiting for transfers between devices, per_device(): lax.all_to_all(outgoing.reshape(row_count, MAXOWN, BLOCK, width), 'row',...  93 us
    while x5, local copies, waits for them, and re-layouts  58.6 us
    dot_general x5, matrix products, first_advance(): jnp.dot(sorter.T, products, precision=lax.Precision.HIGHEST, preferred_el...  55.5 us
    dot_general x2, matrix products, second_advance(): jnp.dot(sorter.T, products, precision=lax.Precision.HIGHEST, preferred_el...  43.7 us
    dot_general x5, matrix products, first_advance(): jnp.einsum('kab,kbo->kao', tile_set, gathered, preferred_element_type=jnp...  36.5 us
    dot_general x2, matrix products, second_advance(): jnp.einsum('kab,kbw->kaw', metric_set, gathered, preferred_element_type=j...  32.4 us
    reduce_scatter x1, waiting for transfers between devices, per_device(): lax.psum_scatter(terms.astype(jnp.bfloat16), 'col', scatter_dimension=0,...  30.7 us
    another operation x1, loops' own time, second_section(): lax.scan(second_advance, start, (metric_sets, slot_sets, out_sets))  14.1 us
  transfers between devices with their start and end apart: 2, of which 2 were waited for; matrix products, arithmetic and copies ran while one was open for 0% of the time, Pallas kernels for 0%

commit v1 on v0

v1 whole, which is shorter than its diff:
```python
import functools
import math

import jax
import jax.numpy as jnp
from jax import lax
from jax.experimental import pallas as pl
from jax.experimental.pallas import tpu as pltpu
from jax.sharding import PartitionSpec as P

BLOCK = 128
OCC = 512
NUW = 2
WIDTH = NUW * OCC
MAXOWN = 2
QB_DEV = 2
PIECES = 2
VMEM_BYTES = 48 << 20


def smem():
    return pl.BlockSpec(memory_space=pltpu.SMEM)


def vmem():
    return pl.BlockSpec(memory_space=pltpu.VMEM)


def params():
    return pltpu.CompilerParams(vmem_limit_bytes=VMEM_BYTES)


def cost(flops, moved):
    return pl.CostEstimate(flops=int(flops), bytes_accessed=int(moved), transcendentals=0)


def write_plan(rows, owner, plan, occ, order, place, moved_flag, start):
    pairs = rows // 2
    i32 = jnp.int32
    for s in range(2 * rows):
        occ[s] = i32(-1)
    for j in range(rows):
        occ[owner[0, j]] = i32(j)
    held = [occ[s] for s in range(2 * rows)]
    has = [(h >= 0).astype(i32) for h in held]
    first_side = sum(has[4 * z] + has[4 * z + 1] for z in range(pairs))
    giver = jnp.where(first_side > pairs, i32(0), i32(1))
    need = jnp.abs(first_side - pairs)
    moved = i32(0)
    counts = [i32(0), i32(0)]
    for z in range(pairs):
        n0 = has[4 * z] + has[4 * z + 1]
        n1 = has[4 * z + 2] + has[4 * z + 3]
        from_count = jnp.where(giver == 0, n0, n1)
        to_count = n0 + n1 - from_count
        move = jnp.logical_and(moved < need, jnp.logical_and(from_count >= 1, to_count <= 1)).astype(i32)
        moved = moved + move
        start[z] = counts[0]
        start[pairs + z] = counts[1]
        for x in range(2):
            for parity in range(2):
                s = 4 * z + 2 * x + parity
                pick = has[s] if parity else has[s] * (1 - has[s + 1])
                chosen = move * pick * jnp.where(giver == x, i32(1), i32(0))
                side = jnp.where(chosen == 1, i32(1 - x), i32(x))
                spot = jnp.where(side == 0, counts[0], counts[1])
                order[jnp.where(has[s] == 1, side * pairs + spot, i32(2 * pairs))] = held[s]
                place[s] = jnp.where(has[s] == 1, spot, i32(-1))
                moved_flag[s] = chosen
                counts[0] = counts[0] + has[s] * (1 - side)
                counts[1] = counts[1] + has[s] * side
    row = lax.axis_index("row")
    z, x = row // 2, row % 2
    lower = z < pairs // 2
    window = jnp.where(lower, 2 * (z + 1), 2 * (pairs - z))
    offset = jnp.where(lower, 0, pairs - window)
    base = jnp.minimum(start[x * pairs + z] - offset, window - 2)
    plan[0] = base
    away = i32(0)
    for parity in range(2):
        s = 4 * z + 2 * (1 - x) + parity
        away = jnp.where(moved_flag[s] == 1, place[s] - offset - base, away)
    plan[1] = away
    for parity in range(2):
        s = 2 * row + parity
        where = jnp.where(moved_flag[s] == 1, i32(2), place[s] - offset - base)
        plan[2 + parity] = jnp.where(place[s] >= 0, where, i32(3))


def first_kernel(rows, table, group, pieces, aux, ao, owner, tiles, coeff, *rest):
    outs, plan = rest[: 2 * pieces], rest[2 * pieces]
    dense, occ, order, place, moved_flag, start = rest[2 * pieces + 1 :]
    pairs = rows // 2
    step = pl.program_id(0)

    @pl.when(step == 0)
    def _():
        write_plan(rows, owner, plan, occ, order, place, moved_flag, start)

        @pl.loop(0, rows * table)
        def _(k):
            dense[k] = jnp.zeros((NUW * BLOCK, BLOCK), jnp.float32)

    @pl.loop(0, group)
    def _(t):
        k = step * group + t
        where = aux[k] * table + ao[k]
        dense[where] += tiles[t].astype(jnp.float32)

    @pl.when(step == pl.num_programs(0) - 1)
    def _():
        x = lax.axis_index("row") % 2
        span = WIDTH // pieces
        for part in range(2):
            side = x if part == 0 else 1 - x

            @pl.loop(0, pairs // 2)
            def _(p):
                for nu in range(NUW):
                    blocks = []
                    for h in range(2):
                        j = order[side * pairs + 2 * p + h]
                        blocks.append(
                            jnp.concatenate(
                                [
                                    dense[j * table + a, pl.ds(nu, BLOCK, stride=NUW), :].astype(jnp.bfloat16)
                                    for a in range(table)
                                ],
                                axis=1,
                            )
                        )
                    left = jnp.concatenate(blocks, axis=0)
                    made = jnp.dot(left, coeff[...], preferred_element_type=jnp.float32).astype(jnp.bfloat16)
                    for h in range(2):
                        for column in range(nu * OCC, (nu + 1) * OCC, min(span, OCC)):
                            piece, inner = column // span, column % span
                            size = min(span, OCC)
                            at = column - nu * OCC
                            outs[2 * piece + part][2 * p + h, :, inner : inner + size] = made[
                                h * BLOCK : (h + 1) * BLOCK, at : at + size
                            ]


def first_section(tiles, aux, ao, owner, coeff, rows, pieces):
    count = tiles.shape[0]
    table = coeff.shape[0] // BLOCK
    group = math.gcd(count, 20)
    pairs = rows // 2
    span = WIDTH // pieces
    piece_shape = jax.ShapeDtypeStruct((pairs, BLOCK, span), jnp.bfloat16)
    whole = pl.BlockSpec((pairs, BLOCK, span), lambda g, *_: (0, 0, 0))
    return pl.pallas_call(
        functools.partial(first_kernel, rows, table, group, pieces),
        grid_spec=pltpu.PrefetchScalarGridSpec(
            num_scalar_prefetch=3,
            grid=(count // group,),
            in_specs=[
                pl.BlockSpec((group, NUW * BLOCK, BLOCK), lambda g, *_: (g, 0, 0)),
                pl.BlockSpec((coeff.shape[0], OCC), lambda g, *_: (0, 0)),
            ],
            out_specs=[whole] * (2 * pieces) + [smem()],
            scratch_shapes=[
                pltpu.VMEM((rows * table, NUW * BLOCK, BLOCK), jnp.float32),
                pltpu.SMEM((2 * rows,), jnp.int32),
                pltpu.SMEM((2 * pairs + 1,), jnp.int32),
                pltpu.SMEM((2 * rows,), jnp.int32),
                pltpu.SMEM((2 * rows,), jnp.int32),
                pltpu.SMEM((2 * pairs,), jnp.int32),
            ],
        ),
        out_shape=[piece_shape] * (2 * pieces) + [jax.ShapeDtypeStruct((4,), jnp.int32)],
        compiler_params=params(),
        cost_estimate=cost(2 * rows * NUW * BLOCK * table * BLOCK * OCC, tiles.size * 2 + coeff.size * 2),
        name="first_section",
    )(aux, ao, owner, tiles, coeff)


def metric_kernel(ys, plan, slots, outs_of, metric, keep, send, dense):
    col = lax.axis_index("col")
    y, core = col // 2, col % 2

    @pl.loop(0, dense.shape[0])
    def _(k):
        dense[k] = jnp.zeros((BLOCK, BLOCK), jnp.float32)

    @pl.loop(0, metric.shape[0])
    def _(k):
        where = outs_of[k] * 4 + plan[2 + slots[k]]
        dense[where] += metric[k].astype(jnp.float32)

    for target, mine in ((keep, core), (send, 1 - core)):
        for d in range(ys):
            to_col = lax.rem(y + d, ys) * 2 + mine
            for h in range(QB_DEV):
                for spot in range(3):
                    target[d, h * BLOCK : (h + 1) * BLOCK, spot * BLOCK : (spot + 1) * BLOCK] = dense[
                        (to_col * QB_DEV + h) * 4 + spot
                    ].astype(jnp.bfloat16)


def metric_section(plan, slots, outs_of, metric, cols):
    ys = cols // 2
    shape = jax.ShapeDtypeStruct((ys, QB_DEV * BLOCK, 3 * BLOCK), jnp.bfloat16)
    return pl.pallas_call(
        functools.partial(metric_kernel, ys),
        in_specs=[smem(), smem(), smem(), vmem()],
        out_specs=[vmem(), vmem()],
        out_shape=[shape, shape],
        scratch_shapes=[pltpu.VMEM((cols * QB_DEV * 4, BLOCK, BLOCK), jnp.float32)],
        compiler_params=params(),
        cost_estimate=cost(0, metric.size * 2 + cols * 400000),
        name="metric_section",
    )(plan, slots, outs_of, metric)


def middle_kernel(pairs, plan, mine, other, own, outward):
    def total(k):
        return (mine[k].astype(jnp.float32) + other[k].astype(jnp.float32)).astype(jnp.bfloat16)

    shift = jnp.where(lax.axis_index("row") // 2 < pairs // 2, 0, 2)
    base = plan[0]
    for k in range(2):
        own[k] = total(base + k)
    for k in range(pairs - 2):
        outward[k] = total(shift + k)


def middle_section(plan, mine, other):
    pairs, _, span = mine.shape
    return pl.pallas_call(
        functools.partial(middle_kernel, pairs),
        in_specs=[smem(), vmem(), vmem()],
        out_specs=[vmem(), vmem()],
        out_shape=[
            jax.ShapeDtypeStruct((2, BLOCK, span), jnp.bfloat16),
            jax.ShapeDtypeStruct((pairs - 2, BLOCK, span), jnp.bfloat16),
        ],
        compiler_params=params(),
        cost_estimate=cost(mine.size, mine.size * 6),
        name="middle_section",
    )(plan, mine, other)


def outward_kernel(pairs, level, plan, own, came, own_out, rest):
    z = lax.axis_index("row") // 2
    lower = z < pairs // 2
    distance = jnp.where(lower, pairs // 2 - 1 - z, z - pairs // 2)
    here = distance == level
    base = plan[0]

    @pl.when(here)
    def _():
        for k in range(2):
            own_out[k] = came[base + k]

    @pl.when(jnp.logical_not(here))
    def _():
        for k in range(2):
            own_out[k] = own[k]

    if level == pairs // 2 - 1:
        rest[0] = own_out[plan[1]]
    else:
        shift = jnp.where(lower, 0, 2)
        for k in range(rest.shape[0]):
            rest[k] = came[shift + k]


def outward_section(plan, own, came, level, pairs):
    span = own.shape[2]
    last = level == pairs // 2 - 1
    return pl.pallas_call(
        functools.partial(outward_kernel, pairs, level),
        in_specs=[smem(), vmem(), vmem()],
        out_specs=[vmem(), vmem()],
        out_shape=[
            jax.ShapeDtypeStruct((2, BLOCK, span), jnp.bfloat16),
            jax.ShapeDtypeStruct((1 if last else came.shape[0] - 2, BLOCK, span), jnp.bfloat16),
        ],
        compiler_params=params(),
        cost_estimate=cost(0, own.size * 8),
        name="outward_section",
    )(plan, own, came)


def term_kernel(ys, keep, got, own, own_core, fix, fix_core, sent, kept):
    span = own.shape[2]
    right = jnp.concatenate(
        [
            own[...].reshape(2 * BLOCK, span),
            fix[0],
            own_core[...].reshape(2 * BLOCK, span),
            fix_core[0],
        ],
        axis=0,
    )
    for d in range(ys - 1, -1, -1):
        left = jnp.concatenate([keep[d], got[d]], axis=1)
        made = jnp.dot(left, right, preferred_element_type=jnp.float32)
        if d:
            sent[d - 1] = made.astype(jnp.bfloat16)
        else:
            kept[...] = made


def term_section(keep, got, own, own_core, fix, fix_core):
    ys = keep.shape[0]
    span = own.shape[2]
    return pl.pallas_call(
        functools.partial(term_kernel, ys),
        in_specs=[vmem()] * 6,
        out_specs=[vmem(), vmem()],
        out_shape=[
            jax.ShapeDtypeStruct((ys - 1, QB_DEV * BLOCK, span), jnp.bfloat16),
            jax.ShapeDtypeStruct((QB_DEV * BLOCK, span), jnp.float32),
        ],
        compiler_params=params(),
        cost_estimate=cost(2 * ys * QB_DEV * BLOCK * 6 * BLOCK * span, keep.size * 4 + span * BLOCK * 24),
        name="term_section",
    )(keep, got, own, own_core, fix, fix_core)


def added(a, b):
    return (a.astype(jnp.float32) + b.astype(jnp.float32)).astype(jnp.bfloat16)


def per_device(
    coeff, tri_blocks, pair_aux, pair_ao, owner_slot, metric_blocks, pair_slot, pair_out
):
    rows = lax.axis_size("row")
    cols = lax.axis_size("col")
    pairs, ys = rows // 2, cols // 2
    half = pairs // 2

    def on_line(moves):
        return [(2 * a + x, 2 * b + x) for a, b in moves for x in range(2)]

    swap_pair = [(r, r ^ 1) for r in range(rows)]
    swap_core = [(c, c ^ 1) for c in range(cols)]

    made = first_section(tri_blocks, pair_aux, pair_ao, owner_slot, coeff, rows, PIECES)
    plan = made[-1]
    keep, send = metric_section(plan, pair_slot, pair_out, metric_blocks, cols)
    got = lax.ppermute(send, "col", swap_core)

    finished = []
    for piece in range(PIECES):
        total = added(made[2 * piece], lax.ppermute(made[2 * piece + 1], "row", swap_pair))
        for a in range(half - 1):
            inward = on_line([(a, a + 1), (pairs - 1 - a, pairs - 2 - a)])
            total = added(total, lax.ppermute(total, "row", inward))
        other = lax.ppermute(total, "row", on_line([(half - 1, half), (half, half - 1)]))
        own, rest = middle_section(plan, total, other)
        for level in range(1, half):
            outward = on_line([(half - level, half - 1 - level), (half - 1 + level, half + level)])
            own, rest = outward_section(plan, own, lax.ppermute(rest, "row", outward), level, pairs)
        fix = lax.ppermute(rest, "row", swap_pair)
        own_core = lax.ppermute(own, "col", swap_core)
        fix_core = lax.ppermute(fix, "col", swap_core)
        sent, kept = term_section(keep, got, own, own_core, fix, fix_core)
        for d in range(1, ys):
            around = [(2 * y + k, 2 * ((y + d) % ys) + k) for y in range(ys) for k in range(2)]
            kept = kept + lax.ppermute(sent[d - 1], "col", around).astype(jnp.float32)
        finished.append(kept.astype(jnp.bfloat16))
    return jnp.concatenate(finished, axis=1)


def solution(mesh):
    in_specs = (
        P("row", None),
        P(("row", "col"), None, None),
        P(("row", "col")),
        P(("row", "col")),
        P("col", None),
        P(("row", "col"), None, None),
        P(("row", "col")),
        P(("row", "col")),
    )
    out_specs = P(("row", "col"), None)
    return jax.shard_map(
        per_device, mesh=mesh, in_specs=in_specs, out_specs=out_specs, check_vma=False
    )
```

time: 422 us -> 97 us (0.23)
  matrix products: 182 us -> 0 us
  waiting for transfers between devices: 124 us -> 52.2 us
  local copies, waits for them, and re-layouts: 72.8 us -> 3.25 us
  Pallas kernels: 0 us -> 17.9 us
  loops' own time: 14.4 us -> 0 us
  starting transfers between devices: 7.44 us -> 21.4 us
  between operations: 13.7 us -> 0.22 us
    dot_general x22 -> x0, matrix products: 182 us -> none  [the longest x5 55.5 us: first_advance(): jnp.dot(sorter.T, products, precision=lax.Precision.HIGHEST, preferred_el...]
    all_to_all x1 -> x0, waiting for transfers between devices: 93 us -> none  [per_device(): lax.all_to_all(outgoing.reshape(row_count, MAXOWN, BLOCK, width), 'row',...]
    while x6 -> x0, local copies, waits for them, and re-layouts: 64.4 us -> none
    ppermute x0 -> x17, waiting for transfers between devices: none -> 52.2 us  [the longest x2 18.8 us: per_device(): lax.ppermute(made[2 * piece + 1], 'row', swap_pair)]
    reduce_scatter x1 -> x0, waiting for transfers between devices: 30.7 us -> none  [per_device(): lax.psum_scatter(terms.astype(jnp.bfloat16), 'col', scatter_dimension=0,...]
    ppermute x0 -> x17, starting transfers between devices: none -> 21.4 us  [the longest x2 7.84 us: per_device(): total = added(total, lax.ppermute(total, 'row', inward))]
    pallas_call x0 -> x8, Pallas kernels: none -> 17.9 us  [the longest x1 12.4 us: first_section(): pl.pallas_call(functools.partial(first_kernel, rows, table, group, pieces...]
    another operation x2 -> x0, loops' own time: 14.4 us -> none  [the longest x1 14.1 us: second_section(): lax.scan(second_advance, start, (metric_sets, slot_sets, out_sets))]
  transfers between devices with their start and end apart: 2 -> 17, of which waited for: 2 -> 10; matrix products, arithmetic and copies ran while one was open for 0% -> 1% of each run, Pallas kernels for 0% -> 6%
where the time goes in v1:
time: 97 us; the launch traced here: 96.6 us
  waiting for transfers between devices  52.2 us (54%)
  starting transfers between devices  21.4 us (22%)
  Pallas kernels  17.9 us (18%)
  local copies, waits for them, and re-layouts  3.25 us (3%)
  other arithmetic  1.6 us (2%)
    ppermute x2, waiting for transfers between devices, per_device(): lax.ppermute(made[2 * piece + 1], 'row', swap_pair)  18.8 us
    pallas_call x1, Pallas kernels, first_section(): pl.pallas_call(functools.partial(first_kernel, rows, table, group, pieces...  12.4 us
    ppermute x2, waiting for transfers between devices, per_device(): total = added(total, lax.ppermute(total, 'row', inward))  9.4 us
    ppermute x2, waiting for transfers between devices, per_device(): lax.ppermute(rest, 'row', outward)  9.35 us
    ppermute x2, starting transfers between devices, per_device(): total = added(total, lax.ppermute(total, 'row', inward))  7.84 us
    ppermute x2, waiting for transfers between devices, per_device(): kept = kept + lax.ppermute(sent[d - 1], 'col', around).astype(jnp.float32)  6.74 us
    ppermute x2, waiting for transfers between devices, per_device(): fix = lax.ppermute(rest, 'row', swap_pair)  6.52 us
    unnamed x14, local copies, waits for them, and re-layouts  3.25 us
  transfers between devices with their start and end apart: 17, of which 10 were waited for; matrix products, arithmetic and copies ran while one was open for 1% of the time, Pallas kernels for 6%

profile of v1, /device:TPU:0, one launch (start us, length us, event | category | flops | bytes accessed | tf_op | source)
XLA Modules:
  0.0 96.6 jit_solution(7171085814322853308)
XLA Ops:
  0.0 0.0 copy-start.1
  0.0 1.2 %copy-done.1 = bf16[1024,512]{1,0:T(8,128)(2,1)S(1)} copy-done((bf16[1024,512]{1,0:T(8,128)(2,1)S(1)}, bf16[1024,512]{1,0:T(8,128)(2,1)}, u32[]{:S(2)}) %copy-start.1) | copy-done | bytes 1048600
  1.2 0.0 copy-start.2
  1.2 0.7 copy-done.2
  1.9 0.0 copy-start.3
  1.9 0.7 copy-done.3
  2.6 0.0 copy-start.4
  2.6 0.7 copy-done.4
  3.2 0.0 copy-start
  3.2 0.0 copy-start.5
  3.2 0.0 copy-start.6
  3.2 12.4 %first_section.1 = (bf16[4,128,512]{2,1,0:T(8,128)(2,1)S(1)}, bf16[4,128,512]{2,1,0:T(8,128)(2,1)S(1)}, bf16[4,128,512]{2,1,0:T(8,128)(2,1)S(1)}, bf16[4,128,512]{2,1,0:T(8,128)(2,1)S(1)}, s32[4]{0:T(128)S(1)}) custom-call(s32[160]{0:T(256)S(1)} %copy-done.2, s32[160]{0:T(256)S(1)} %copy-done.3, s32[1,8]{1,0:T(1,128)S(1)} %copy-done.4, ...), custom_call_target="tpu_custom_call" | custom-call | flops 2147483648 | bytes 11534336 | tf_op jit(solution)/shard_map/first_section/pallas_call | solution.py:152
  15.7 3.0 %collective-permute-start.9 = (bf16[4,128,512]{2,1,0:T(8,128)(2,1)S(1)}, bf16[4,128,512]{2,1,0:T(8,128)(2,1)S(1)}, u32[]{:S(2)}, u32[]{:S(2)}) collective-permute-start(bf16[4,128,512]{2,1,0:T(8,128)(2,1)S(1)} %get-tuple-element.36), channel_id=1, source_target_pairs={{0,4},{4,0},{8,12},{12,8},{16,20},{20,16},{24,28},{28,24},{1,5},{5... | collective-permute-start | bytes 1572872 | tf_op jit(solution)/shard_map/ppermute | solution.py:348
  18.7 0.1 collective-permute-start.1
  18.7 12.7 %collective-permute-done.9 = bf16[4,128,512]{2,1,0:T(8,128)(2,1)S(1)} collective-permute-done((bf16[4,128,512]{2,1,0:T(8,128)(2,1)S(1)}, bf16[4,128,512]{2,1,0:T(8,128)(2,1)S(1)}, u32[]{:S(2)}, u32[]{:S(2)}) %collective-permute-start.9) | collective-permute-done | bytes 524320 | tf_op jit(solution)/shard_map/ppermute | solution.py:348
  31.4 0.1 add_convert_fusion.1
  31.6 4.1 %collective-permute-start.10 = (bf16[4,128,512]{2,1,0:T(8,128)(2,1)S(1)}, bf16[4,128,512]{2,1,0:T(8,128)(2,1)S(1)}, u32[]{:S(2)}, u32[]{:S(2)}) collective-permute-start(bf16[4,128,512]{2,1,0:T(8,128)(2,1)S(1)} %add_convert_fusion.1), channel_id=1, source_target_pairs={{0,8},{4,12},{24,16},{28,20},{1,9},{5,13},{25,17},{29,21},{2,10},{... | collective-permute-start | bytes 1572872 | tf_op jit(solution)/shard_map/ppermute | solution.py:351
  35.7 6.2 %collective-permute-done.1 = bf16[4,128,512]{2,1,0:T(8,128)(2,1)S(1)} collective-permute-done((bf16[4,128,512]{2,1,0:T(8,128)(2,1)S(1)}, bf16[4,128,512]{2,1,0:T(8,128)(2,1)S(1)}, u32[]{:S(2)}, u32[]{:S(2)}) %collective-permute-start.1) | collective-permute-done | bytes 524320 | tf_op jit(solution)/shard_map/ppermute | solution.py:348
  41.8 0.1 add_convert_fusion.3
  42.0 3.8 %collective-permute-start.2 = (bf16[4,128,512]{2,1,0:T(8,128)(2,1)S(1)}, bf16[4,128,512]{2,1,0:T(8,128)(2,1)S(1)}, u32[]{:S(2)}, u32[]{:S(2)}) collective-permute-start(bf16[4,128,512]{2,1,0:T(8,128)(2,1)S(1)} %add_convert_fusion.3), channel_id=1, source_target_pairs={{0,8},{4,12},{24,16},{28,20},{1,9},{5,13},{25,17},{29,21},{2,10},{... | collective-permute-start | bytes 1572872 | tf_op jit(solution)/shard_map/ppermute | solution.py:351
  45.7 0.0 collective-permute-done.10
  45.7 0.1 add_convert_fusion.mine
  45.9 0.7 collective-permute-start.11
  46.6 9.4 %collective-permute-done.2 = bf16[4,128,512]{2,1,0:T(8,128)(2,1)S(1)} collective-permute-done((bf16[4,128,512]{2,1,0:T(8,128)(2,1)S(1)}, bf16[4,128,512]{2,1,0:T(8,128)(2,1)S(1)}, u32[]{:S(2)}, u32[]{:S(2)}) %collective-permute-start.2) | collective-permute-done | bytes 524320 | tf_op jit(solution)/shard_map/ppermute | solution.py:351
  56.0 0.1 add_convert_fusion.2.mine
  56.1 0.7 collective-permute-start.3
  56.8 0.0 collective-permute-done.11.other
  56.9 0.7 middle_section.3
  57.5 1.3 %collective-permute-start.12 = (bf16[2,128,512]{2,1,0:T(8,128)(2,1)S(1)}, bf16[2,128,512]{2,1,0:T(8,128)(2,1)S(1)}, u32[]{:S(2)}, u32[]{:S(2)}) collective-permute-start(bf16[2,128,512]{2,1,0:T(8,128)(2,1)S(1)} %get-tuple-element.38), channel_id=1, source_target_pairs={{8,0},{12,4},{16,24},{20,28},{9,1},{13,5},{17,25},{21,29},{10,2},{... | collective-permute-start | bytes 786440 | tf_op jit(solution)/shard_map/ppermute | solution.py:356
  58.8 0.0 copy-done
  58.8 0.0 copy-done.5
  58.8 0.0 copy-done.6
  58.9 1.8 %metric_section.1 = (bf16[2,256,384]{2,1,0:T(8,128)(2,1)S(1)}, bf16[2,256,384]{2,1,0:T(8,128)(2,1)S(1)}) custom-call(s32[4]{0:T(128)S(1)} %get-tuple-element.24.plan, s32[64]{0:T(128)S(1)} %copy-done.5, s32[64]{0:T(128)S(1)} %copy-done.6, bf16[64,128,128]{2,1,0:T(8,128)(2,1)S(1)} %copy-done), custom_call_target="tpu_custom_call" | custom-call | bytes 3697152 | tf_op jit(solution)/shard_map/metric_section/pallas_call | solution.py:204
  60.7 0.1 collective-permute-start
  60.7 0.0 collective-permute-done.3.other
  60.8 0.7 middle_section.2
  61.4 1.3 %collective-permute-start.4 = (bf16[2,128,512]{2,1,0:T(8,128)(2,1)S(1)}, bf16[2,128,512]{2,1,0:T(8,128)(2,1)S(1)}, u32[]{:S(2)}, u32[]{:S(2)}) collective-permute-start(bf16[2,128,512]{2,1,0:T(8,128)(2,1)S(1)} %get-tuple-element.30), channel_id=1, source_target_pairs={{8,0},{12,4},{16,24},{20,28},{9,1},{13,5},{17,25},{21,29},{10,2},{... | collective-permute-start | bytes 786440 | tf_op jit(solution)/shard_map/ppermute | solution.py:356
  62.7 5.7 %collective-permute-done.12.came = bf16[2,128,512]{2,1,0:T(8,128)(2,1)S(1)} collective-permute-done((bf16[2,128,512]{2,1,0:T(8,128)(2,1)S(1)}, bf16[2,128,512]{2,1,0:T(8,128)(2,1)S(1)}, u32[]{:S(2)}, u32[]{:S(2)}) %collective-permute-start.12) | collective-permute-done | bytes 262176 | tf_op jit(solution)/shard_map/ppermute | solution.py:356
  68.4 0.6 outward_section.3
  69.0 0.1 collective-permute-start.13
  69.1 1.6 %collective-permute-start.14 = (bf16[1,128,512]{2,1,0:T(8,128)(2,1)S(1)}, bf16[1,128,512]{2,1,0:T(8,128)(2,1)S(1)}, u32[]{:S(2)}, u32[]{:S(2)}) collective-permute-start(bf16[1,128,512]{2,1,0:T(8,128)(2,1)S(1)} %get-tuple-element.40), channel_id=1, source_target_pairs={{0,4},{4,0},{8,12},{12,8},{16,20},{20,16},{24,28},{28,24},{1,5},{5... | collective-permute-start | bytes 393224 | tf_op jit(solution)/shard_map/ppermute | solution.py:357
  70.7 4.3 %collective-permute-done.14.fix = bf16[1,128,512]{2,1,0:T(8,128)(2,1)S(1)} collective-permute-done((bf16[1,128,512]{2,1,0:T(8,128)(2,1)S(1)}, bf16[1,128,512]{2,1,0:T(8,128)(2,1)S(1)}, u32[]{:S(2)}, u32[]{:S(2)}) %collective-permute-start.14) | collective-permute-done | bytes 131104 | tf_op jit(solution)/shard_map/ppermute | solution.py:357
  75.0 0.0 collective-permute-start.15
  75.0 3.7 %collective-permute-done.4.came = bf16[2,128,512]{2,1,0:T(8,128)(2,1)S(1)} collective-permute-done((bf16[2,128,512]{2,1,0:T(8,128)(2,1)S(1)}, bf16[2,128,512]{2,1,0:T(8,128)(2,1)S(1)}, u32[]{:S(2)}, u32[]{:S(2)}) %collective-permute-start.4) | collective-permute-done | bytes 262176 | tf_op jit(solution)/shard_map/ppermute | solution.py:356
  78.7 0.6 outward_section.2
  79.3 0.1 collective-permute-start.5
  79.4 1.6 %collective-permute-start.6 = (bf16[1,128,512]{2,1,0:T(8,128)(2,1)S(1)}, bf16[1,128,512]{2,1,0:T(8,128)(2,1)S(1)}, u32[]{:S(2)}, u32[]{:S(2)}) collective-permute-start(bf16[1,128,512]{2,1,0:T(8,128)(2,1)S(1)} %get-tuple-element.32), channel_id=1, source_target_pairs={{0,4},{4,0},{8,12},{12,8},{16,20},{20,16},{24,28},{28,24},{1,5},{5... | collective-permute-start | bytes 393224 | tf_op jit(solution)/shard_map/ppermute | solution.py:357
  80.9 0.0 collective-permute-done.got
  80.9 0.0 collective-permute-done.13.own_core
  80.9 0.0 collective-permute-done.15.fix_core
  80.9 0.6 term_section.3
  81.5 1.6 %collective-permute-start.16 = (bf16[256,512]{1,0:T(8,128)(2,1)S(1)}, bf16[256,512]{1,0:T(8,128)(2,1)S(1)}, u32[]{:S(2)}, u32[]{:S(2)}) collective-permute-start(bf16[256,512]{1,0:T(8,128)(2,1)S(1)} %bitcast.2), channel_id=1, source_target_pairs={{0,2},{1,3},{2,0},{3,1},{4,6},{5,7},{6,4},{7,5},{8,10},{9,11},{10,... | collective-permute-start | bytes 786440 | tf_op jit(solution)/shard_map/ppermute | solution.py:363
  83.1 2.2 %collective-permute-done.6.fix = bf16[1,128,512]{2,1,0:T(8,128)(2,1)S(1)} collective-permute-done((bf16[1,128,512]{2,1,0:T(8,128)(2,1)S(1)}, bf16[1,128,512]{2,1,0:T(8,128)(2,1)S(1)}, u32[]{:S(2)}, u32[]{:S(2)}) %collective-permute-start.6) | collective-permute-done | bytes 131104 | tf_op jit(solution)/shard_map/ppermute | solution.py:357
  85.3 0.0 collective-permute-start.7
  85.3 0.0 collective-permute-done.5.own_core
  85.3 1.3 %collective-permute-done.7.fix_core = bf16[1,128,512]{2,1,0:T(8,128)(2,1)S(1)} collective-permute-done((bf16[1,128,512]{2,1,0:T(8,128)(2,1)S(1)}, bf16[1,128,512]{2,1,0:T(8,128)(2,1)S(1)}, u32[]{:S(2)}, u32[]{:S(2)}) %collective-permute-start.7) | collective-permute-done | bytes 131104 | tf_op jit(solution)/shard_map/ppermute | solution.py:359
  86.6 0.6 term_section.2
  87.2 1.6 %collective-permute-start.8 = (bf16[256,512]{1,0:T(8,128)(2,1)S(1)}, bf16[256,512]{1,0:T(8,128)(2,1)S(1)}, u32[]{:S(2)}, u32[]{:S(2)}) collective-permute-start(bf16[256,512]{1,0:T(8,128)(2,1)S(1)} %bitcast.3), channel_id=1, source_target_pairs={{0,2},{1,3},{2,0},{3,1},{4,6},{5,7},{6,4},{7,5},{8,10},{9,11},{10,... | collective-permute-start | bytes 786440 | tf_op jit(solution)/shard_map/ppermute | solution.py:363
  88.8 1.2 %collective-permute-done.16 = bf16[256,512]{1,0:T(8,128)(2,1)S(1)} collective-permute-done((bf16[256,512]{1,0:T(8,128)(2,1)S(1)}, bf16[256,512]{1,0:T(8,128)(2,1)S(1)}, u32[]{:S(2)}, u32[]{:S(2)}) %collective-permute-start.16) | collective-permute-done | bytes 262176 | tf_op jit(solution)/shard_map/ppermute | solution.py:363
  90.0 0.1 add_convert_fusion.4
  90.0 5.6 %collective-permute-done.8 = bf16[256,512]{1,0:T(8,128)(2,1)S(1)} collective-permute-done((bf16[256,512]{1,0:T(8,128)(2,1)S(1)}, bf16[256,512]{1,0:T(8,128)(2,1)S(1)}, u32[]{:S(2)}, u32[]{:S(2)}) %collective-permute-start.8) | collective-permute-done | bytes 262176 | tf_op jit(solution)/shard_map/ppermute | solution.py:363
  95.6 0.1 add_convert_fusion.5
  95.7 0.9 pad_maximum_fusion
Async XLA Ops:
  0.0 1.2 %copy-start.1 = (bf16[1024,512]{1,0:T(8,128)(2,1)S(1)}, bf16[1024,512]{1,0:T(8,128)(2,1)}, u32[]{:S(2)}) copy-start(bf16[1024,512]{1,0:T(8,128)(2,1)} %coeff.1) | copy-start | bytes 3145732
  1.2 0.7 copy-start.2
  1.9 0.7 copy-start.3
  2.6 0.7 copy-start.4
  3.2 55.6 %copy-start = (bf16[64,128,128]{2,1,0:T(8,128)(2,1)S(1)}, bf16[64,128,128]{2,1,0:T(8,128)(2,1)}, u32[]{:S(2)}) copy-start(bf16[64,128,128]{2,1,0:T(8,128)(2,1)} %metric.1) | copy-start | bytes 6291460
  3.2 55.6 %copy-start.5 = (s32[64]{0:T(128)S(1)}, s32[64]{0:T(128)}, u32[]{:S(2)}) copy-start(s32[64]{0:T(128)} %slots.1) | copy-start | bytes 772
  3.2 55.6 %copy-start.6 = (s32[64]{0:T(128)S(1)}, s32[64]{0:T(128)}, u32[]{:S(2)}) copy-start(s32[64]{0:T(128)} %outs_of.1) | copy-start | bytes 772
  15.7 15.8 %collective-permute-start.9 = (bf16[4,128,512]{2,1,0:T(8,128)(2,1)S(1)}, bf16[4,128,512]{2,1,0:T(8,128)(2,1)S(1)}, u32[]{:S(2)}, u32[]{:S(2)}) collective-permute-start(bf16[4,128,512]{2,1,0:T(8,128)(2,1)S(1)} %get-tuple-element.36), channel_id=1, source_target_pairs={{0,4},{4,0},{8,12},{12,8},{16,20},{20,16},{24,28},{28,24},{1,5},{5... | collective-permute-start | bytes 1572872 | tf_op jit(solution)/shard_map/ppermute | solution.py:348
  18.7 23.2 %collective-permute-start.1 = (bf16[4,128,512]{2,1,0:T(8,128)(2,1)S(1)}, bf16[4,128,512]{2,1,0:T(8,128)(2,1)S(1)}, u32[]{:S(2)}, u32[]{:S(2)}) collective-permute-start(bf16[4,128,512]{2,1,0:T(8,128)(2,1)S(1)} %get-tuple-element.28), channel_id=1, source_target_pairs={{0,4},{4,0},{8,12},{12,8},{16,20},{20,16},{24,28},{28,24},{1,5},{5... | collective-permute-start | bytes 1572872 | tf_op jit(solution)/shard_map/ppermute | solution.py:348
  31.6 14.2 %collective-permute-start.10 = (bf16[4,128,512]{2,1,0:T(8,128)(2,1)S(1)}, bf16[4,128,512]{2,1,0:T(8,128)(2,1)S(1)}, u32[]{:S(2)}, u32[]{:S(2)}) collective-permute-start(bf16[4,128,512]{2,1,0:T(8,128)(2,1)S(1)} %add_convert_fusion.1), channel_id=1, source_target_pairs={{0,8},{4,12},{24,16},{28,20},{1,9},{5,13},{25,17},{29,21},{2,10},{... | collective-permute-start | bytes 1572872 | tf_op jit(solution)/shard_map/ppermute | solution.py:351
  42.0 14.0 %collective-permute-start.2 = (bf16[4,128,512]{2,1,0:T(8,128)(2,1)S(1)}, bf16[4,128,512]{2,1,0:T(8,128)(2,1)S(1)}, u32[]{:S(2)}, u32[]{:S(2)}) collective-permute-start(bf16[4,128,512]{2,1,0:T(8,128)(2,1)S(1)} %add_convert_fusion.3), channel_id=1, source_target_pairs={{0,8},{4,12},{24,16},{28,20},{1,9},{5,13},{25,17},{29,21},{2,10},{... | collective-permute-start | bytes 1572872 | tf_op jit(solution)/shard_map/ppermute | solution.py:351
  45.9 10.9 %collective-permute-start.11 = (bf16[4,128,512]{2,1,0:T(8,128)(2,1)S(1)}, bf16[4,128,512]{2,1,0:T(8,128)(2,1)S(1)}, u32[]{:S(2)}, u32[]{:S(2)}) collective-permute-start(bf16[4,128,512]{2,1,0:T(8,128)(2,1)S(1)} %add_convert_fusion.mine), channel_id=1, source_target_pairs={{8,16},{12,20},{16,8},{20,12},{9,17},{13,21},{17,9},{21,13},{10,18... | collective-permute-start | bytes 1572872 | tf_op jit(solution)/shard_map/ppermute | solution.py:352
  56.1 4.6 %collective-permute-start.3 = (bf16[4,128,512]{2,1,0:T(8,128)(2,1)S(1)}, bf16[4,128,512]{2,1,0:T(8,128)(2,1)S(1)}, u32[]{:S(2)}, u32[]{:S(2)}) collective-permute-start(bf16[4,128,512]{2,1,0:T(8,128)(2,1)S(1)} %add_convert_fusion.2.mine), channel_id=1, source_target_pairs={{8,16},{12,20},{16,8},{20,12},{9,17},{13,21},{17,9},{21,13},{10,18... | collective-permute-start | bytes 1572872 | tf_op jit(solution)/shard_map/ppermute | solution.py:352
  57.5 10.9 %collective-permute-start.12 = (bf16[2,128,512]{2,1,0:T(8,128)(2,1)S(1)}, bf16[2,128,512]{2,1,0:T(8,128)(2,1)S(1)}, u32[]{:S(2)}, u32[]{:S(2)}) collective-permute-start(bf16[2,128,512]{2,1,0:T(8,128)(2,1)S(1)} %get-tuple-element.38), channel_id=1, source_target_pairs={{8,0},{12,4},{16,24},{20,28},{9,1},{13,5},{17,25},{21,29},{10,2},{... | collective-permute-start | bytes 786440 | tf_op jit(solution)/shard_map/ppermute | solution.py:356
  60.7 20.3 %collective-permute-start = (bf16[2,256,384]{2,1,0:T(8,128)(2,1)S(1)}, bf16[2,256,384]{2,1,0:T(8,128)(2,1)S(1)}, u32[]{:S(2)}, u32[]{:S(2)}) collective-permute-start(bf16[2,256,384]{2,1,0:T(8,128)(2,1)S(1)} %get-tuple-element.26), channel_id=1, source_target_pairs={{0,1},{1,0},{2,3},{3,2},{4,5},{5,4},{6,7},{7,6},{8,9},{9,8},{10,11... | collective-permute-start | bytes 1179656 | tf_op jit(solution)/shard_map/ppermute | solution.py:344
  61.4 17.2 %collective-permute-start.4 = (bf16[2,128,512]{2,1,0:T(8,128)(2,1)S(1)}, bf16[2,128,512]{2,1,0:T(8,128)(2,1)S(1)}, u32[]{:S(2)}, u32[]{:S(2)}) collective-permute-start(bf16[2,128,512]{2,1,0:T(8,128)(2,1)S(1)} %get-tuple-element.30), channel_id=1, source_target_pairs={{8,0},{12,4},{16,24},{20,28},{9,1},{13,5},{17,25},{21,29},{10,2},{... | collective-permute-start | bytes 786440 | tf_op jit(solution)/shard_map/ppermute | solution.py:356
  69.0 11.9 %collective-permute-start.13 = (bf16[2,128,512]{2,1,0:T(8,128)(2,1)S(1)}, bf16[2,128,512]{2,1,0:T(8,128)(2,1)S(1)}, u32[]{:S(2)}, u32[]{:S(2)}) collective-permute-start(bf16[2,128,512]{2,1,0:T(8,128)(2,1)S(1)} %get-tuple-element.39.own), channel_id=1, source_target_pairs={{0,1},{1,0},{2,3},{3,2},{4,5},{5,4},{6,7},{7,6},{8,9},{9,8},{10,11... | collective-permute-start | bytes 786440 | tf_op jit(solution)/shard_map/ppermute | solution.py:358
  69.1 5.9 %collective-permute-start.14 = (bf16[1,128,512]{2,1,0:T(8,128)(2,1)S(1)}, bf16[1,128,512]{2,1,0:T(8,128)(2,1)S(1)}, u32[]{:S(2)}, u32[]{:S(2)}) collective-permute-start(bf16[1,128,512]{2,1,0:T(8,128)(2,1)S(1)} %get-tuple-element.40), channel_id=1, source_target_pairs={{0,4},{4,0},{8,12},{12,8},{16,20},{20,16},{24,28},{28,24},{1,5},{5... | collective-permute-start | bytes 393224 | tf_op jit(solution)/shard_map/ppermute | solution.py:357
  75.0 5.9 %collective-permute-start.15 = (bf16[1,128,512]{2,1,0:T(8,128)(2,1)S(1)}, bf16[1,128,512]{2,1,0:T(8,128)(2,1)S(1)}, u32[]{:S(2)}, u32[]{:S(2)}) collective-permute-start(bf16[1,128,512]{2,1,0:T(8,128)(2,1)S(1)} %collective-permute-done.14.fix), channel_id=1, source_target_pairs={{0,1},{1,0},{2,3},{3,2},{4,5},{5,4},{6,7},{7,6},{8,9},{9,8},{10,11... | collective-permute-start | bytes 393224 | tf_op jit(solution)/shard_map/ppermute | solution.py:359
  79.3 6.0 %collective-permute-start.5 = (bf16[2,128,512]{2,1,0:T(8,128)(2,1)S(1)}, bf16[2,128,512]{2,1,0:T(8,128)(2,1)S(1)}, u32[]{:S(2)}, u32[]{:S(2)}) collective-permute-start(bf16[2,128,512]{2,1,0:T(8,128)(2,1)S(1)} %get-tuple-element.31.own), channel_id=1, source_target_pairs={{0,1},{1,0},{2,3},{3,2},{4,5},{5,4},{6,7},{7,6},{8,9},{9,8},{10,11... | collective-permute-start | bytes 786440 | tf_op jit(solution)/shard_map/ppermute | solution.py:358
  79.4 5.9 %collective-permute-start.6 = (bf16[1,128,512]{2,1,0:T(8,128)(2,1)S(1)}, bf16[1,128,512]{2,1,0:T(8,128)(2,1)S(1)}, u32[]{:S(2)}, u32[]{:S(2)}) collective-permute-start(bf16[1,128,512]{2,1,0:T(8,128)(2,1)S(1)} %get-tuple-element.32), channel_id=1, source_target_pairs={{0,4},{4,0},{8,12},{12,8},{16,20},{20,16},{24,28},{28,24},{1,5},{5... | collective-permute-start | bytes 393224 | tf_op jit(solution)/shard_map/ppermute | solution.py:357
  81.5 8.4 %collective-permute-start.16 = (bf16[256,512]{1,0:T(8,128)(2,1)S(1)}, bf16[256,512]{1,0:T(8,128)(2,1)S(1)}, u32[]{:S(2)}, u32[]{:S(2)}) collective-permute-start(bf16[256,512]{1,0:T(8,128)(2,1)S(1)} %bitcast.2), channel_id=1, source_target_pairs={{0,2},{1,3},{2,0},{3,1},{4,6},{5,7},{6,4},{7,5},{8,10},{9,11},{10,... | collective-permute-start | bytes 786440 | tf_op jit(solution)/shard_map/ppermute | solution.py:363
  85.3 1.3 %collective-permute-start.7 = (bf16[1,128,512]{2,1,0:T(8,128)(2,1)S(1)}, bf16[1,128,512]{2,1,0:T(8,128)(2,1)S(1)}, u32[]{:S(2)}, u32[]{:S(2)}) collective-permute-start(bf16[1,128,512]{2,1,0:T(8,128)(2,1)S(1)} %collective-permute-done.6.fix), channel_id=1, source_target_pairs={{0,1},{1,0},{2,3},{3,2},{4,5},{5,4},{6,7},{7,6},{8,9},{9,8},{10,11... | collective-permute-start | bytes 393224 | tf_op jit(solution)/shard_map/ppermute | solution.py:359
  87.2 8.4 %collective-permute-start.8 = (bf16[256,512]{1,0:T(8,128)(2,1)S(1)}, bf16[256,512]{1,0:T(8,128)(2,1)S(1)}, u32[]{:S(2)}, u32[]{:S(2)}) collective-permute-start(bf16[256,512]{1,0:T(8,128)(2,1)S(1)} %bitcast.3), channel_id=1, source_target_pairs={{0,2},{1,3},{2,0},{3,1},{4,6},{5,7},{6,4},{7,5},{8,10},{9,11},{10,... | collective-permute-start | bytes 786440 | tf_op jit(solution)/shard_map/ppermute | solution.py:363

commit v2 on v1

--- a/solution.py
+++ b/solution.py
@@ -11,11 +11,9 @@
 BLOCK = 128
 OCC = 512
 NUW = 2
-WIDTH = NUW * OCC
 MAXOWN = 2
 QB_DEV = 2
-PIECES = 2
-VMEM_BYTES = 48 << 20
+SMALL_VMEM = 8 << 20
 
 
 def smem():
@@ -26,8 +24,8 @@
     return pl.BlockSpec(memory_space=pltpu.VMEM)
 
 
-def params():
-    return pltpu.CompilerParams(vmem_limit_bytes=VMEM_BYTES)
+def params(limit=SMALL_VMEM):
+    return pltpu.CompilerParams(vmem_limit_bytes=limit)
 
 
 def cost(flops, moved):
@@ -87,92 +85,140 @@
         plan[2 + parity] = jnp.where(place[s] >= 0, where, i32(3))
 
 
-def first_kernel(rows, table, group, pieces, aux, ao, owner, tiles, coeff, *rest):
-    outs, plan = rest[: 2 * pieces], rest[2 * pieces]
-    dense, occ, order, place, moved_flag, start = rest[2 * pieces + 1 :]
+def first_kernel(
+    rows, table, group, aux_in, ao_in, owner_in, tiles_in, coeff_in, keep, send, plan, later,
+    tiles, coeff, dense, made, left_later, aux, ao, owner, occ, order, place, moved_flag, start, sems, out_sems,
+):
     pairs = rows // 2
-    step = pl.program_id(0)
-
-    @pl.when(step == 0)
-    def _():
-        write_plan(rows, owner, plan, occ, order, place, moved_flag, start)
-
-        @pl.loop(0, rows * table)
-        def _(k):
-            dense[k] = jnp.zeros((NUW * BLOCK, BLOCK), jnp.float32)
-
-    @pl.loop(0, group)
-    def _(t):
-        k = step * group + t
-        where = aux[k] * table + ao[k]
-        dense[where] += tiles[t].astype(jnp.float32)
-
-    @pl.when(step == pl.num_programs(0) - 1)
-    def _():
-        x = lax.axis_index("row") % 2
-        span = WIDTH // pieces
-        for part in range(2):
-            side = x if part == 0 else 1 - x
-
-            @pl.loop(0, pairs // 2)
-            def _(p):
-                for nu in range(NUW):
-                    blocks = []
-                    for h in range(2):
-                        j = order[side * pairs + 2 * p + h]
-                        blocks.append(
-                            jnp.concatenate(
-                                [
-                                    dense[j * table + a, pl.ds(nu, BLOCK, stride=NUW), :].astype(jnp.bfloat16)
-                                    for a in range(table)
-                                ],
-                                axis=1,
-                            )
+    groups = tiles.shape[0]
+    small = [
+        pltpu.make_async_copy(aux_in, aux, sems.at[groups]),
+        pltpu.make_async_copy(ao_in, ao, sems.at[groups + 1]),
+        pltpu.make_async_copy(owner_in, owner, sems.at[groups + 2]),
+    ]
+    loads = [
+        pltpu.make_async_copy(tiles_in.at[pl.ds(g * group, group)], tiles.at[g], sems.at[g]) for g in range(groups)
+    ]
+    table_load = pltpu.make_async_copy(coeff_in, coeff, sems.at[groups + 3])
+    for copy in (*small, *loads, table_load):
+        copy.start()
+
+    @pl.loop(0, rows * table, unroll=4)
+    def _(k):
+        dense[k] = jnp.zeros((NUW * BLOCK, BLOCK), jnp.float32)
+
+    for copy in small:
+        copy.wait()
+    write_plan(rows, owner, plan, occ, order, place, moved_flag, start)
+
+    for g in range(groups):
+        loads[g].wait()
+
+        @pl.loop(0, group, unroll=4)
+        def _(t):
+            k = g * group + t
+            where = aux[k] * table + ao[k]
+            dense[where] += tiles[g, t].astype(jnp.float32)
+
+    table_load.wait()
+    x = lax.axis_index("row") % 2
+    stores = []
+    for part, out in ((1, send), (0, keep)):
+        side = x if part == 0 else 1 - x
+        for p in range(pairs // 2):
+            at = part * pairs + 2 * p
+            for nu in range(NUW):
+                blocks = []
+                for h in range(2):
+                    j = order[side * pairs + 2 * p + h]
+                    blocks.append(
+                        jnp.concatenate(
+                            [
+                                dense[j * table + a, pl.ds(nu, BLOCK, stride=NUW), :].astype(jnp.bfloat16)
+                                for a in range(table)
+                            ],
+                            axis=1,
                         )
-                    left = jnp.concatenate(blocks, axis=0)
-                    made = jnp.dot(left, coeff[...], preferred_element_type=jnp.float32).astype(jnp.bfloat16)
-                    for h in range(2):
-                        for column in range(nu * OCC, (nu + 1) * OCC, min(span, OCC)):
-                            piece, inner = column // span, column % span
-                            size = min(span, OCC)
-                            at = column - nu * OCC
-                            outs[2 * piece + part][2 * p + h, :, inner : inner + size] = made[
-                                h * BLOCK : (h + 1) * BLOCK, at : at + size
-                            ]
-
-
-def first_section(tiles, aux, ao, owner, coeff, rows, pieces):
+                    )
+                left = jnp.concatenate(blocks, axis=0)
+                if nu:
+                    left_later[at : at + 2] = left.reshape(2, BLOCK, table * BLOCK)
+                    stores.append((left_later.at[pl.ds(at, 2)], later.at[pl.ds(at, 2)]))
+                else:
+                    value = jnp.dot(left, coeff[...], preferred_element_type=jnp.float32)
+                    made[at : at + 2] = value.astype(jnp.bfloat16).reshape(2, BLOCK, OCC)
+                    stores.append((made.at[pl.ds(at, 2)], out.at[pl.ds(2 * p, 2)]))
+                stores[-1] = pltpu.make_async_copy(*stores[-1], out_sems.at[len(stores) - 1])
+                stores[-1].start()
+    for copy in stores:
+        copy.wait()
+
+
+def first_section(tiles, aux, ao, owner, coeff, rows):
     count = tiles.shape[0]
     table = coeff.shape[0] // BLOCK
     group = math.gcd(count, 20)
+    groups = count // group
     pairs = rows // 2
-    span = WIDTH // pieces
-    piece_shape = jax.ShapeDtypeStruct((pairs, BLOCK, span), jnp.bfloat16)
-    whole = pl.BlockSpec((pairs, BLOCK, span), lambda g, *_: (0, 0, 0))
-    return pl.pallas_call(
-        functools.partial(first_kernel, rows, table, group, pieces),
-        grid_spec=pltpu.PrefetchScalarGridSpec(
-            num_scalar_prefetch=3,
-            grid=(count // group,),
-            in_specs=[
-                pl.BlockSpec((group, NUW * BLOCK, BLOCK), lambda g, *_: (g, 0, 0)),
-                pl.BlockSpec((coeff.shape[0], OCC), lambda g, *_: (0, 0)),
-            ],
-            out_specs=[whole] * (2 * pieces) + [smem()],
-            scratch_shapes=[
-                pltpu.VMEM((rows * table, NUW * BLOCK, BLOCK), jnp.float32),
-                pltpu.SMEM((2 * rows,), jnp.int32),
-                pltpu.SMEM((2 * pairs + 1,), jnp.int32),
-                pltpu.SMEM((2 * rows,), jnp.int32),
-                pltpu.SMEM((2 * rows,), jnp.int32),
-                pltpu.SMEM((2 * pairs,), jnp.int32),
-            ],
-        ),
-        out_shape=[piece_shape] * (2 * pieces) + [jax.ShapeDtypeStruct((4,), jnp.int32)],
-        compiler_params=params(),
-        cost_estimate=cost(2 * rows * NUW * BLOCK * table * BLOCK * OCC, tiles.size * 2 + coeff.size * 2),
+    any_space = pl.BlockSpec(memory_space=pl.ANY)
+    half = jax.ShapeDtypeStruct((pairs, BLOCK, OCC), jnp.bfloat16)
+    held = 2 * tiles.size + 2 * coeff.size + rows * table * NUW * BLOCK * BLOCK * 4 + rows * BLOCK * 4 * OCC * 2
+    return pl.pallas_call(
+        functools.partial(first_kernel, rows, table, group),
+        in_specs=[any_space] * 5,
+        out_specs=[any_space, any_space, smem(), any_space],
+        out_shape=[
+            half,
+            half,
+            jax.ShapeDtypeStruct((4 + pairs,), jnp.int32),
+            jax.ShapeDtypeStruct((rows, BLOCK, table * BLOCK), jnp.bfloat16),
+        ],
+        scratch_shapes=[
+            pltpu.VMEM((groups, group, NUW * BLOCK, BLOCK), jnp.bfloat16),
+            pltpu.VMEM(coeff.shape, jnp.bfloat16),
+            pltpu.VMEM((rows * table, NUW * BLOCK, BLOCK), jnp.float32),
+            pltpu.VMEM((rows, BLOCK, OCC), jnp.bfloat16),
+            pltpu.VMEM((rows, BLOCK, table * BLOCK), jnp.bfloat16),
+            pltpu.SMEM((count,), jnp.int32),
+            pltpu.SMEM((count,), jnp.int32),
+            pltpu.SMEM(owner.shape, jnp.int32),
+            pltpu.SMEM((2 * rows,), jnp.int32),
+            pltpu.SMEM((2 * pairs + 1,), jnp.int32),
+            pltpu.SMEM((2 * rows,), jnp.int32),
+            pltpu.SMEM((2 * rows,), jnp.int32),
+            pltpu.SMEM((2 * pairs,), jnp.int32),
+            pltpu.SemaphoreType.DMA((groups + 4,)),
+            pltpu.SemaphoreType.DMA((NUW * pairs,)),
+        ],
+        compiler_params=params(max(held + (8 << 20), 56 << 20)),
+        cost_estimate=cost(rows * NUW * BLOCK * table * BLOCK * OCC, tiles.size * 2 + coeff.size * 2),
         name="first_section",
     )(aux, ao, owner, tiles, coeff)
+
+
+def later_kernel(left, coeff, keep, send):
+    pairs, _, span = keep.shape
+    for part, out in ((1, send), (0, keep)):
+        for p in range(0, pairs, 2):
+            at = part * pairs + p
+            value = jnp.dot(
+                left[at : at + 2].reshape(2 * BLOCK, left.shape[2]), coeff[...], preferred_element_type=jnp.float32
+            )
+            out[p : p + 2] = value.astype(jnp.bfloat16).reshape(2, BLOCK, span)
+
+
+def later_section(left, coeff):
+    rows = left.shape[0]
+    half = jax.ShapeDtypeStruct((rows // 2, BLOCK, OCC), jnp.bfloat16)
+    return pl.pallas_call(
+        later_kernel,
+        in_specs=[vmem(), vmem()],
+        out_specs=[vmem(), vmem()],
+        out_shape=[half, half],
+        compiler_params=params(2 * SMALL_VMEM),
+        cost_estimate=cost(left.size * 2 * OCC, left.size * 4),
+        name="later_section",
+    )(left, coeff)
 
 
 def metric_kernel(ys, plan, slots, outs_of, metric, keep, send, dense):
@@ -207,7 +253,7 @@
         out_specs=[vmem(), vmem()],
         out_shape=[shape, shape],
         scratch_shapes=[pltpu.VMEM((cols * QB_DEV * 4, BLOCK, BLOCK), jnp.float32)],
-        compiler_params=params(),
+        compiler_params=params(2 * SMALL_VMEM),
         cost_estimate=cost(0, metric.size * 2 + cols * 400000),
         name="metric_section",
     )(plan, slots, outs_of, metric)
@@ -338,13 +384,13 @@
     swap_pair = [(r, r ^ 1) for r in range(rows)]
     swap_core = [(c, c ^ 1) for c in range(cols)]
 
-    made = first_section(tri_blocks, pair_aux, pair_ao, owner_slot, coeff, rows, PIECES)
-    plan = made[-1]
+    *early, plan, left = first_section(tri_blocks, pair_aux, pair_ao, owner_slot, coeff, rows)
+    made = (*early, *later_section(left, coeff))
     keep, send = metric_section(plan, pair_slot, pair_out, metric_blocks, cols)
     got = lax.ppermute(send, "col", swap_core)
 
     finished = []
-    for piece in range(PIECES):
+    for piece in range(NUW):
         total = added(made[2 * piece], lax.ppermute(made[2 * piece + 1], "row", swap_pair))
         for a in range(half - 1):
             inward = on_line([(a, a + 1), (pairs - 1 - a, pairs - 2 - a)])

time: 97 us -> 89.2 us (0.920)
  Pallas kernels: 17.9 us -> 14.3 us
  waiting for transfers between devices: 52.2 us -> 49.6 us
  local copies, waits for them, and re-layouts: 3.25 us -> 1.62 us
    pallas_call x1 -> x2, Pallas kernels: 12.4 us -> 8.88 us  [the longest x1 7.64 us: first_section(): pl.pallas_call(functools.partial(first_kernel, rows, table, group), in_sp...]
    ppermute x2, waiting for transfers between devices: 18.8 us -> 16.2 us  [per_device(): lax.ppermute(made[2 * piece + 1], 'row', swap_pair)]
    unnamed x14, local copies, waits for them, and re-layouts: 3.25 us -> 1.62 us
  transfers between devices with their start and end apart: 17 -> 17, of which waited for: 10 -> 10; matrix products, arithmetic and copies ran while one was open for 1% -> 1% of each run, Pallas kernels for 6% -> 8%
where the time goes in v2:
time: 89.2 us; the launch traced here: 88.9 us
  waiting for transfers between devices  49.6 us (56%)
  starting transfers between devices  21.5 us (24%)
  Pallas kernels  14.3 us (16%)
  local copies, waits for them, and re-layouts  1.62 us (2%)
  other arithmetic  1.56 us (2%)
    ppermute x2, waiting for transfers between devices, per_device(): lax.ppermute(made[2 * piece + 1], 'row', swap_pair)  16.2 us
    ppermute x2, waiting for transfers between devices, per_device(): total = added(total, lax.ppermute(total, 'row', inward))  9.41 us
    ppermute x2, waiting for transfers between devices, per_device(): lax.ppermute(rest, 'row', outward)  9.35 us
    ppermute x2, starting transfers between devices, per_device(): total = added(total, lax.ppermute(total, 'row', inward))  7.97 us
    pallas_call x1, Pallas kernels, first_section(): pl.pallas_call(functools.partial(first_kernel, rows, table, group), in_sp...  7.64 us
    ppermute x2, waiting for transfers between devices, per_device(): kept = kept + lax.ppermute(sent[d - 1], 'col', around).astype(jnp.float32)  6.77 us
    ppermute x2, waiting for transfers between devices, per_device(): fix = lax.ppermute(rest, 'row', swap_pair)  6.55 us
    ppermute x2, starting transfers between devices, per_device(): kept = kept + lax.ppermute(sent[d - 1], 'col', around).astype(jnp.float32)  3.16 us
  transfers between devices with their start and end apart: 17, of which 10 were waited for; matrix products, arithmetic and copies ran while one was open for 1% of the time, Pallas kernels for 8%

profile of v2, /device:TPU:0, one launch (start us, length us, event | category | flops | bytes accessed | tf_op | source)
XLA Modules:
  0.0 88.9 jit_solution(16220698823230752776)
XLA Ops:
  0.0 0.0 copy-start.1
  0.0 7.6 %first_section.1 = (bf16[4,128,512]{2,1,0:T(8,128)(2,1)}, bf16[4,128,512]{2,1,0:T(8,128)(2,1)}, s32[8]{0:T(128)}, bf16[8,128,1024]{2,1,0:T(8,128)(2,1)}) custom-call(s32[160]{0:T(256)} %aux_in.1, s32[160]{0:T(256)} %ao_in.1, s32[1,8]{1,0:T(1,128)} %owner_in.1, bf16[160,256,128]{2,1,0:T(8,128)(2,1)} %tiles_in.1, bf16[1024,512]{1,0:T(8,128)(2,1)} %coeff.1), custom_call_target="tpu_custom_call" | custom-call | flops 1073741824 | bytes 11534336 | tf_op jit(solution)/shard_map/first_section/pallas_call | solution.py:166
  7.6 3.0 %collective-permute-start.1 = (bf16[4,128,512]{2,1,0:T(8,128)(2,1)}, bf16[4,128,512]{2,1,0:T(8,128)(2,1)S(1)}, u32[]{:S(2)}, u32[]{:S(2)}) collective-permute-start(bf16[4,128,512]{2,1,0:T(8,128)(2,1)} %get-tuple-element.29), channel_id=1, source_target_pairs={{0,4},{4,0},{8,12},{12,8},{16,20},{20,16},{24,28},{28,24},{1,5},{5... | collective-permute-start | bytes 1572872 | tf_op jit(solution)/shard_map/ppermute | solution.py:394
  10.7 0.0 copy-done.1
  10.7 0.0 copy-start.5
  10.7 1.6 %copy-done.5 = bf16[8,128,1024]{2,1,0:T(8,128)(2,1)S(1)} copy-done((bf16[8,128,1024]{2,1,0:T(8,128)(2,1)S(1)}, bf16[8,128,1024]{2,1,0:T(8,128)(2,1)}, u32[]{:S(2)}) %copy-start.5) | copy-done | bytes 2097176
  12.2 0.0 copy-start.6
  12.3 1.2 %later_section.1 = (bf16[4,128,512]{2,1,0:T(8,128)(2,1)S(1)}, bf16[4,128,512]{2,1,0:T(8,128)(2,1)S(1)}) custom-call(bf16[8,128,1024]{2,1,0:T(8,128)(2,1)S(1)} %copy-done.5, bf16[1024,512]{1,0:T(8,128)(2,1)S(1)} %copy-done.1), custom_call_target="tpu_custom_call" | custom-call | flops 1073741824 | bytes 4194304 | tf_op jit(solution)/shard_map/later_section/pallas_call | solution.py:213
  13.5 0.1 collective-permute-start.9
  13.6 10.0 %collective-permute-done.1 = bf16[4,128,512]{2,1,0:T(8,128)(2,1)S(1)} collective-permute-done((bf16[4,128,512]{2,1,0:T(8,128)(2,1)}, bf16[4,128,512]{2,1,0:T(8,128)(2,1)S(1)}, u32[]{:S(2)}, u32[]{:S(2)}) %collective-permute-start.1) | collective-permute-done | bytes 524320 | tf_op jit(solution)/shard_map/ppermute | solution.py:394
  23.6 0.0 copy-done.6
  23.6 0.1 add_convert_fusion.3
  23.8 4.1 %collective-permute-start.2 = (bf16[4,128,512]{2,1,0:T(8,128)(2,1)S(1)}, bf16[4,128,512]{2,1,0:T(8,128)(2,1)S(1)}, u32[]{:S(2)}, u32[]{:S(2)}) collective-permute-start(bf16[4,128,512]{2,1,0:T(8,128)(2,1)S(1)} %add_convert_fusion.3), channel_id=1, source_target_pairs={{0,8},{4,12},{24,16},{28,20},{1,9},{5,13},{25,17},{29,21},{2,10},{... | collective-permute-start | bytes 1572872 | tf_op jit(solution)/shard_map/ppermute | solution.py:397
  27.8 6.2 %collective-permute-done.9 = bf16[4,128,512]{2,1,0:T(8,128)(2,1)S(1)} collective-permute-done((bf16[4,128,512]{2,1,0:T(8,128)(2,1)S(1)}, bf16[4,128,512]{2,1,0:T(8,128)(2,1)S(1)}, u32[]{:S(2)}, u32[]{:S(2)}) %collective-permute-start.9) | collective-permute-done | bytes 524320 | tf_op jit(solution)/shard_map/ppermute | solution.py:394
  34.0 0.0 copy-start.2
  34.0 0.1 add_convert_fusion.1
  34.2 0.0 copy-start
  34.2 0.0 copy-start.3
  34.2 0.0 copy-start.4
  34.2 3.9 %collective-permute-start.10 = (bf16[4,128,512]{2,1,0:T(8,128)(2,1)S(1)}, bf16[4,128,512]{2,1,0:T(8,128)(2,1)S(1)}, u32[]{:S(2)}, u32[]{:S(2)}) collective-permute-start(bf16[4,128,512]{2,1,0:T(8,128)(2,1)S(1)} %add_convert_fusion.1), channel_id=1, source_target_pairs={{0,8},{4,12},{24,16},{28,20},{1,9},{5,13},{25,17},{29,21},{2,10},{... | collective-permute-start | bytes 1572872 | tf_op jit(solution)/shard_map/ppermute | solution.py:397
  38.1 0.0 collective-permute-done.2
  38.1 0.1 add_convert_fusion.2.mine
  38.3 0.7 collective-permute-start.3
  39.0 9.4 %collective-permute-done.10 = bf16[4,128,512]{2,1,0:T(8,128)(2,1)S(1)} collective-permute-done((bf16[4,128,512]{2,1,0:T(8,128)(2,1)S(1)}, bf16[4,128,512]{2,1,0:T(8,128)(2,1)S(1)}, u32[]{:S(2)}, u32[]{:S(2)}) %collective-permute-start.10) | collective-permute-done | bytes 524320 | tf_op jit(solution)/shard_map/ppermute | solution.py:397
  48.4 0.1 add_convert_fusion.mine
  48.5 0.7 collective-permute-start.11
  49.2 0.0 collective-permute-done.3.other
  49.2 0.0 copy-done.2
  49.2 0.7 middle_section.2
  49.9 1.3 %collective-permute-start.4 = (bf16[2,128,512]{2,1,0:T(8,128)(2,1)S(1)}, bf16[2,128,512]{2,1,0:T(8,128)(2,1)S(1)}, u32[]{:S(2)}, u32[]{:S(2)}) collective-permute-start(bf16[2,128,512]{2,1,0:T(8,128)(2,1)S(1)} %get-tuple-element.31), channel_id=1, source_target_pairs={{8,0},{12,4},{16,24},{20,28},{9,1},{13,5},{17,25},{21,29},{10,2},{... | collective-permute-start | bytes 786440 | tf_op jit(solution)/shard_map/ppermute | solution.py:402
  51.2 0.0 copy-done
  51.2 0.0 copy-done.3
  51.2 0.0 copy-done.4
  51.2 1.8 %metric_section.1 = (bf16[2,256,384]{2,1,0:T(8,128)(2,1)S(1)}, bf16[2,256,384]{2,1,0:T(8,128)(2,1)S(1)}) custom-call(s32[8]{0:T(128)S(1)} %copy-done.2, s32[64]{0:T(128)S(1)} %copy-done.3, s32[64]{0:T(128)S(1)} %copy-done.4, bf16[64,128,128]{2,1,0:T(8,128)(2,1)S(1)} %copy-done), custom_call_target="tpu_custom_call" | custom-call | bytes 3697152 | tf_op jit(solution)/shard_map/metric_section/pallas_call | solution.py:250
  53.0 0.1 collective-permute-start
  53.1 0.0 collective-permute-done.11.other
  53.1 0.7 middle_section.3
  53.8 1.3 %collective-permute-start.12 = (bf16[2,128,512]{2,1,0:T(8,128)(2,1)S(1)}, bf16[2,128,512]{2,1,0:T(8,128)(2,1)S(1)}, u32[]{:S(2)}, u32[]{:S(2)}) collective-permute-start(bf16[2,128,512]{2,1,0:T(8,128)(2,1)S(1)} %get-tuple-element.40), channel_id=1, source_target_pairs={{8,0},{12,4},{16,24},{20,28},{9,1},{13,5},{17,25},{21,29},{10,2},{... | collective-permute-start | bytes 786440 | tf_op jit(solution)/shard_map/ppermute | solution.py:402
  55.1 5.7 %collective-permute-done.4.came = bf16[2,128,512]{2,1,0:T(8,128)(2,1)S(1)} collective-permute-done((bf16[2,128,512]{2,1,0:T(8,128)(2,1)S(1)}, bf16[2,128,512]{2,1,0:T(8,128)(2,1)S(1)}, u32[]{:S(2)}, u32[]{:S(2)}) %collective-permute-start.4) | collective-permute-done | bytes 262176 | tf_op jit(solution)/shard_map/ppermute | solution.py:402
  60.8 0.6 outward_section.2
  61.4 0.1 collective-permute-start.5
  61.5 1.6 %collective-permute-start.6 = (bf16[1,128,512]{2,1,0:T(8,128)(2,1)S(1)}, bf16[1,128,512]{2,1,0:T(8,128)(2,1)S(1)}, u32[]{:S(2)}, u32[]{:S(2)}) collective-permute-start(bf16[1,128,512]{2,1,0:T(8,128)(2,1)S(1)} %get-tuple-element.33), channel_id=1, source_target_pairs={{0,4},{4,0},{8,12},{12,8},{16,20},{20,16},{24,28},{28,24},{1,5},{5... | collective-permute-start | bytes 393224 | tf_op jit(solution)/shard_map/ppermute | solution.py:403
  63.0 4.4 %collective-permute-done.6.fix = bf16[1,128,512]{2,1,0:T(8,128)(2,1)S(1)} collective-permute-done((bf16[1,128,512]{2,1,0:T(8,128)(2,1)S(1)}, bf16[1,128,512]{2,1,0:T(8,128)(2,1)S(1)}, u32[]{:S(2)}, u32[]{:S(2)}) %collective-permute-start.6) | collective-permute-done | bytes 131104 | tf_op jit(solution)/shard_map/ppermute | solution.py:403
  67.4 0.0 collective-permute-start.7
  67.4 3.7 %collective-permute-done.12.came = bf16[2,128,512]{2,1,0:T(8,128)(2,1)S(1)} collective-permute-done((bf16[2,128,512]{2,1,0:T(8,128)(2,1)S(1)}, bf16[2,128,512]{2,1,0:T(8,128)(2,1)S(1)}, u32[]{:S(2)}, u32[]{:S(2)}) %collective-permute-start.12) | collective-permute-done | bytes 262176 | tf_op jit(solution)/shard_map/ppermute | solution.py:402
  71.0 0.6 outward_section.3
  71.6 0.1 collective-permute-start.13
  71.7 1.5 %collective-permute-start.14 = (bf16[1,128,512]{2,1,0:T(8,128)(2,1)S(1)}, bf16[1,128,512]{2,1,0:T(8,128)(2,1)S(1)}, u32[]{:S(2)}, u32[]{:S(2)}) collective-permute-start(bf16[1,128,512]{2,1,0:T(8,128)(2,1)S(1)} %get-tuple-element.42), channel_id=1, source_target_pairs={{0,4},{4,0},{8,12},{12,8},{16,20},{20,16},{24,28},{28,24},{1,5},{5... | collective-permute-start | bytes 393224 | tf_op jit(solution)/shard_map/ppermute | solution.py:403
  73.3 0.0 collective-permute-done.got
  73.3 0.0 collective-permute-done.5.own_core
  73.3 0.0 collective-permute-done.7.fix_core
  73.3 0.6 term_section.2
  73.9 1.6 %collective-permute-start.8 = (bf16[256,512]{1,0:T(8,128)(2,1)S(1)}, bf16[256,512]{1,0:T(8,128)(2,1)S(1)}, u32[]{:S(2)}, u32[]{:S(2)}) collective-permute-start(bf16[256,512]{1,0:T(8,128)(2,1)S(1)} %bitcast.2), channel_id=1, source_target_pairs={{0,2},{1,3},{2,0},{3,1},{4,6},{5,7},{6,4},{7,5},{8,10},{9,11},{10,... | collective-permute-start | bytes 786440 | tf_op jit(solution)/shard_map/ppermute | solution.py:409
  75.4 2.2 %collective-permute-done.14.fix = bf16[1,128,512]{2,1,0:T(8,128)(2,1)S(1)} collective-permute-done((bf16[1,128,512]{2,1,0:T(8,128)(2,1)S(1)}, bf16[1,128,512]{2,1,0:T(8,128)(2,1)S(1)}, u32[]{:S(2)}, u32[]{:S(2)}) %collective-permute-start.14) | collective-permute-done | bytes 131104 | tf_op jit(solution)/shard_map/ppermute | solution.py:403
  77.6 0.0 collective-permute-start.15
  77.6 0.0 collective-permute-done.13.own_core
  77.6 1.3 %collective-permute-done.15.fix_core = bf16[1,128,512]{2,1,0:T(8,128)(2,1)S(1)} collective-permute-done((bf16[1,128,512]{2,1,0:T(8,128)(2,1)S(1)}, bf16[1,128,512]{2,1,0:T(8,128)(2,1)S(1)}, u32[]{:S(2)}, u32[]{:S(2)}) %collective-permute-start.15) | collective-permute-done | bytes 131104 | tf_op jit(solution)/shard_map/ppermute | solution.py:405
  79.0 0.6 term_section.3
  79.6 1.6 %collective-permute-start.16 = (bf16[256,512]{1,0:T(8,128)(2,1)S(1)}, bf16[256,512]{1,0:T(8,128)(2,1)S(1)}, u32[]{:S(2)}, u32[]{:S(2)}) collective-permute-start(bf16[256,512]{1,0:T(8,128)(2,1)S(1)} %bitcast.3), channel_id=1, source_target_pairs={{0,2},{1,3},{2,0},{3,1},{4,6},{5,7},{6,4},{7,5},{8,10},{9,11},{10,... | collective-permute-start | bytes 786440 | tf_op jit(solution)/shard_map/ppermute | solution.py:409
  81.1 1.2 %collective-permute-done.8 = bf16[256,512]{1,0:T(8,128)(2,1)S(1)} collective-permute-done((bf16[256,512]{1,0:T(8,128)(2,1)S(1)}, bf16[256,512]{1,0:T(8,128)(2,1)S(1)}, u32[]{:S(2)}, u32[]{:S(2)}) %collective-permute-start.8) | collective-permute-done | bytes 262176 | tf_op jit(solution)/shard_map/ppermute | solution.py:409
  82.3 0.1 add_convert_fusion.5
  82.4 5.6 %collective-permute-done.16 = bf16[256,512]{1,0:T(8,128)(2,1)S(1)} collective-permute-done((bf16[256,512]{1,0:T(8,128)(2,1)S(1)}, bf16[256,512]{1,0:T(8,128)(2,1)S(1)}, u32[]{:S(2)}, u32[]{:S(2)}) %collective-permute-start.16) | collective-permute-done | bytes 262176 | tf_op jit(solution)/shard_map/ppermute | solution.py:409
  88.0 0.1 add_convert_fusion.4
  88.1 0.9 pad_maximum_fusion
Async XLA Ops:
  0.0 10.7 %copy-start.1 = (bf16[1024,512]{1,0:T(8,128)(2,1)S(1)}, bf16[1024,512]{1,0:T(8,128)(2,1)}, u32[]{:S(2)}) copy-start(bf16[1024,512]{1,0:T(8,128)(2,1)} %coeff.1) | copy-start | bytes 3145732
  7.6 16.0 %collective-permute-start.1 = (bf16[4,128,512]{2,1,0:T(8,128)(2,1)}, bf16[4,128,512]{2,1,0:T(8,128)(2,1)S(1)}, u32[]{:S(2)}, u32[]{:S(2)}) collective-permute-start(bf16[4,128,512]{2,1,0:T(8,128)(2,1)} %get-tuple-element.29), channel_id=1, source_target_pairs={{0,4},{4,0},{8,12},{12,8},{16,20},{20,16},{24,28},{28,24},{1,5},{5... | collective-permute-start | bytes 1572872 | tf_op jit(solution)/shard_map/ppermute | solution.py:394
  10.7 1.6 %copy-start.5 = (bf16[8,128,1024]{2,1,0:T(8,128)(2,1)S(1)}, bf16[8,128,1024]{2,1,0:T(8,128)(2,1)}, u32[]{:S(2)}) copy-start(bf16[8,128,1024]{2,1,0:T(8,128)(2,1)} %get-tuple-element.36.left) | copy-start | bytes 6291460
  12.2 11.4 %copy-start.6 = (bf16[4,128,512]{2,1,0:T(8,128)(2,1)S(1)}, bf16[4,128,512]{2,1,0:T(8,128)(2,1)}, u32[]{:S(2)}) copy-start(bf16[4,128,512]{2,1,0:T(8,128)(2,1)} %get-tuple-element.28) | copy-start | bytes 1572868
  13.5 20.5 %collective-permute-start.9 = (bf16[4,128,512]{2,1,0:T(8,128)(2,1)S(1)}, bf16[4,128,512]{2,1,0:T(8,128)(2,1)S(1)}, u32[]{:S(2)}, u32[]{:S(2)}) collective-permute-start(bf16[4,128,512]{2,1,0:T(8,128)(2,1)S(1)} %get-tuple-element.38), channel_id=1, source_target_pairs={{0,4},{4,0},{8,12},{12,8},{16,20},{20,16},{24,28},{28,24},{1,5},{5... | collective-permute-start | bytes 1572872 | tf_op jit(solution)/shard_map/ppermute | solution.py:394
  23.8 14.3 %collective-permute-start.2 = (bf16[4,128,512]{2,1,0:T(8,128)(2,1)S(1)}, bf16[4,128,512]{2,1,0:T(8,128)(2,1)S(1)}, u32[]{:S(2)}, u32[]{:S(2)}) collective-permute-start(bf16[4,128,512]{2,1,0:T(8,128)(2,1)S(1)} %add_convert_fusion.3), channel_id=1, source_target_pairs={{0,8},{4,12},{24,16},{28,20},{1,9},{5,13},{25,17},{29,21},{2,10},{... | collective-permute-start | bytes 1572872 | tf_op jit(solution)/shard_map/ppermute | solution.py:397
  34.0 15.2 %copy-start.2 = (s32[8]{0:T(128)S(1)}, s32[8]{0:T(128)}, u32[]{:S(2)}) copy-start(s32[8]{0:T(128)} %get-tuple-element.25.plan) | copy-start | bytes 100
  34.2 17.0 %copy-start = (bf16[64,128,128]{2,1,0:T(8,128)(2,1)S(1)}, bf16[64,128,128]{2,1,0:T(8,128)(2,1)}, u32[]{:S(2)}) copy-start(bf16[64,128,128]{2,1,0:T(8,128)(2,1)} %metric.1) | copy-start | bytes 6291460
  34.2 17.0 %copy-start.3 = (s32[64]{0:T(128)S(1)}, s32[64]{0:T(128)}, u32[]{:S(2)}) copy-start(s32[64]{0:T(128)} %slots.1) | copy-start | bytes 772
  34.2 17.0 %copy-start.4 = (s32[64]{0:T(128)S(1)}, s32[64]{0:T(128)}, u32[]{:S(2)}) copy-start(s32[64]{0:T(128)} %outs_of.1) | copy-start | bytes 772
  34.2 14.2 %collective-permute-start.10 = (bf16[4,128,512]{2,1,0:T(8,128)(2,1)S(1)}, bf16[4,128,512]{2,1,0:T(8,128)(2,1)S(1)}, u32[]{:S(2)}, u32[]{:S(2)}) collective-permute-start(bf16[4,128,512]{2,1,0:T(8,128)(2,1)S(1)} %add_convert_fusion.1), channel_id=1, source_target_pairs={{0,8},{4,12},{24,16},{28,20},{1,9},{5,13},{25,17},{29,21},{2,10},{... | collective-permute-start | bytes 1572872 | tf_op jit(solution)/shard_map/ppermute | solution.py:397
  38.3 10.9 %collective-permute-start.3 = (bf16[4,128,512]{2,1,0:T(8,128)(2,1)S(1)}, bf16[4,128,512]{2,1,0:T(8,128)(2,1)S(1)}, u32[]{:S(2)}, u32[]{:S(2)}) collective-permute-start(bf16[4,128,512]{2,1,0:T(8,128)(2,1)S(1)} %add_convert_fusion.2.mine), channel_id=1, source_target_pairs={{8,16},{12,20},{16,8},{20,12},{9,17},{13,21},{17,9},{21,13},{10,18... | collective-permute-start | bytes 1572872 | tf_op jit(solution)/shard_map/ppermute | solution.py:398
  48.5 4.6 %collective-permute-start.11 = (bf16[4,128,512]{2,1,0:T(8,128)(2,1)S(1)}, bf16[4,128,512]{2,1,0:T(8,128)(2,1)S(1)}, u32[]{:S(2)}, u32[]{:S(2)}) collective-permute-start(bf16[4,128,512]{2,1,0:T(8,128)(2,1)S(1)} %add_convert_fusion.mine), channel_id=1, source_target_pairs={{8,16},{12,20},{16,8},{20,12},{9,17},{13,21},{17,9},{21,13},{10,18... | collective-permute-start | bytes 1572872 | tf_op jit(solution)/shard_map/ppermute | solution.py:398
  49.9 10.9 %collective-permute-start.4 = (bf16[2,128,512]{2,1,0:T(8,128)(2,1)S(1)}, bf16[2,128,512]{2,1,0:T(8,128)(2,1)S(1)}, u32[]{:S(2)}, u32[]{:S(2)}) collective-permute-start(bf16[2,128,512]{2,1,0:T(8,128)(2,1)S(1)} %get-tuple-element.31), channel_id=1, source_target_pairs={{8,0},{12,4},{16,24},{20,28},{9,1},{13,5},{17,25},{21,29},{10,2},{... | collective-permute-start | bytes 786440 | tf_op jit(solution)/shard_map/ppermute | solution.py:402
  53.0 20.2 %collective-permute-start = (bf16[2,256,384]{2,1,0:T(8,128)(2,1)S(1)}, bf16[2,256,384]{2,1,0:T(8,128)(2,1)S(1)}, u32[]{:S(2)}, u32[]{:S(2)}) collective-permute-start(bf16[2,256,384]{2,1,0:T(8,128)(2,1)S(1)} %get-tuple-element.27), channel_id=1, source_target_pairs={{0,1},{1,0},{2,3},{3,2},{4,5},{5,4},{6,7},{7,6},{8,9},{9,8},{10,11... | collective-permute-start | bytes 1179656 | tf_op jit(solution)/shard_map/ppermute | solution.py:390
  53.8 17.2 %collective-permute-start.12 = (bf16[2,128,512]{2,1,0:T(8,128)(2,1)S(1)}, bf16[2,128,512]{2,1,0:T(8,128)(2,1)S(1)}, u32[]{:S(2)}, u32[]{:S(2)}) collective-permute-start(bf16[2,128,512]{2,1,0:T(8,128)(2,1)S(1)} %get-tuple-element.40), channel_id=1, source_target_pairs={{8,0},{12,4},{16,24},{20,28},{9,1},{13,5},{17,25},{21,29},{10,2},{... | collective-permute-start | bytes 786440 | tf_op jit(solution)/shard_map/ppermute | solution.py:402
  61.4 11.9 %collective-permute-start.5 = (bf16[2,128,512]{2,1,0:T(8,128)(2,1)S(1)}, bf16[2,128,512]{2,1,0:T(8,128)(2,1)S(1)}, u32[]{:S(2)}, u32[]{:S(2)}) collective-permute-start(bf16[2,128,512]{2,1,0:T(8,128)(2,1)S(1)} %get-tuple-element.32.own), channel_id=1, source_target_pairs={{0,1},{1,0},{2,3},{3,2},{4,5},{5,4},{6,7},{7,6},{8,9},{9,8},{10,11... | collective-permute-start | bytes 786440 | tf_op jit(solution)/shard_map/ppermute | solution.py:404
  61.5 5.9 %collective-permute-start.6 = (bf16[1,128,512]{2,1,0:T(8,128)(2,1)S(1)}, bf16[1,128,512]{2,1,0:T(8,128)(2,1)S(1)}, u32[]{:S(2)}, u32[]{:S(2)}) collective-permute-start(bf16[1,128,512]{2,1,0:T(8,128)(2,1)S(1)} %get-tuple-element.33), channel_id=1, source_target_pairs={{0,4},{4,0},{8,12},{12,8},{16,20},{20,16},{24,28},{28,24},{1,5},{5... | collective-permute-start | bytes 393224 | tf_op jit(solution)/shard_map/ppermute | solution.py:403
  67.4 5.9 %collective-permute-start.7 = (bf16[1,128,512]{2,1,0:T(8,128)(2,1)S(1)}, bf16[1,128,512]{2,1,0:T(8,128)(2,1)S(1)}, u32[]{:S(2)}, u32[]{:S(2)}) collective-permute-start(bf16[1,128,512]{2,1,0:T(8,128)(2,1)S(1)} %collective-permute-done.6.fix), channel_id=1, source_target_pairs={{0,1},{1,0},{2,3},{3,2},{4,5},{5,4},{6,7},{7,6},{8,9},{9,8},{10,11... | collective-permute-start | bytes 393224 | tf_op jit(solution)/shard_map/ppermute | solution.py:405
  71.6 6.0 %collective-permute-start.13 = (bf16[2,128,512]{2,1,0:T(8,128)(2,1)S(1)}, bf16[2,128,512]{2,1,0:T(8,128)(2,1)S(1)}, u32[]{:S(2)}, u32[]{:S(2)}) collective-permute-start(bf16[2,128,512]{2,1,0:T(8,128)(2,1)S(1)} %get-tuple-element.41.own), channel_id=1, source_target_pairs={{0,1},{1,0},{2,3},{3,2},{4,5},{5,4},{6,7},{7,6},{8,9},{9,8},{10,11... | collective-permute-start | bytes 786440 | tf_op jit(solution)/shard_map/ppermute | solution.py:404
  71.7 5.9 %collective-permute-start.14 = (bf16[1,128,512]{2,1,0:T(8,128)(2,1)S(1)}, bf16[1,128,512]{2,1,0:T(8,128)(2,1)S(1)}, u32[]{:S(2)}, u32[]{:S(2)}) collective-permute-start(bf16[1,128,512]{2,1,0:T(8,128)(2,1)S(1)} %get-tuple-element.42), channel_id=1, source_target_pairs={{0,4},{4,0},{8,12},{12,8},{16,20},{20,16},{24,28},{28,24},{1,5},{5... | collective-permute-start | bytes 393224 | tf_op jit(solution)/shard_map/ppermute | solution.py:403
  73.9 8.4 %collective-permute-start.8 = (bf16[256,512]{1,0:T(8,128)(2,1)S(1)}, bf16[256,512]{1,0:T(8,128)(2,1)S(1)}, u32[]{:S(2)}, u32[]{:S(2)}) collective-permute-start(bf16[256,512]{1,0:T(8,128)(2,1)S(1)} %bitcast.2), channel_id=1, source_target_pairs={{0,2},{1,3},{2,0},{3,1},{4,6},{5,7},{6,4},{7,5},{8,10},{9,11},{10,... | collective-permute-start | bytes 786440 | tf_op jit(solution)/shard_map/ppermute | solution.py:409
  77.6 1.3 %collective-permute-start.15 = (bf16[1,128,512]{2,1,0:T(8,128)(2,1)S(1)}, bf16[1,128,512]{2,1,0:T(8,128)(2,1)S(1)}, u32[]{:S(2)}, u32[]{:S(2)}) collective-permute-start(bf16[1,128,512]{2,1,0:T(8,128)(2,1)S(1)} %collective-permute-done.14.fix), channel_id=1, source_target_pairs={{0,1},{1,0},{2,3},{3,2},{4,5},{5,4},{6,7},{7,6},{8,9},{9,8},{10,11... | collective-permute-start | bytes 393224 | tf_op jit(solution)/shard_map/ppermute | solution.py:405
  79.6 8.4 %collective-permute-start.16 = (bf16[256,512]{1,0:T(8,128)(2,1)S(1)}, bf16[256,512]{1,0:T(8,128)(2,1)S(1)}, u32[]{:S(2)}, u32[]{:S(2)}) collective-permute-start(bf16[256,512]{1,0:T(8,128)(2,1)S(1)} %bitcast.3), channel_id=1, source_target_pairs={{0,2},{1,3},{2,0},{3,1},{4,6},{5,7},{6,4},{7,5},{8,10},{9,11},{10,... | collective-permute-start | bytes 786440 | tf_op jit(solution)/shard_map/ppermute | solution.py:409

commit v3 on v2

--- a/solution.py
+++ b/solution.py
@@ -69,20 +69,17 @@
                 counts[1] = counts[1] + has[s] * side
     row = lax.axis_index("row")
     z, x = row // 2, row % 2
-    lower = z < pairs // 2
-    window = jnp.where(lower, 2 * (z + 1), 2 * (pairs - z))
-    offset = jnp.where(lower, 0, pairs - window)
-    base = jnp.minimum(start[x * pairs + z] - offset, window - 2)
-    plan[0] = base
+    base = jnp.minimum(start[x * pairs + z], pairs - 2)
     away = i32(0)
     for parity in range(2):
         s = 4 * z + 2 * (1 - x) + parity
-        away = jnp.where(moved_flag[s] == 1, place[s] - offset - base, away)
-    plan[1] = away
+        away = jnp.where(moved_flag[s] == 1, place[s] - base, away)
+    plan[0] = away
     for parity in range(2):
         s = 2 * row + parity
-        where = jnp.where(moved_flag[s] == 1, i32(2), place[s] - offset - base)
-        plan[2 + parity] = jnp.where(place[s] >= 0, where, i32(3))
+        where = jnp.where(moved_flag[s] == 1, i32(2), place[s] - base)
+        plan[1 + parity] = jnp.where(place[s] >= 0, where, i32(3))
+    plan[3] = base
 
 
 def first_kernel(
@@ -170,7 +167,7 @@
         out_shape=[
             half,
             half,
-            jax.ShapeDtypeStruct((4 + pairs,), jnp.int32),
+            jax.ShapeDtypeStruct((4,), jnp.int32),
             jax.ShapeDtypeStruct((rows, BLOCK, table * BLOCK), jnp.bfloat16),
         ],
         scratch_shapes=[
@@ -231,7 +228,7 @@
 
     @pl.loop(0, metric.shape[0])
     def _(k):
-        where = outs_of[k] * 4 + plan[2 + slots[k]]
+        where = outs_of[k] * 4 + plan[1 + slots[k]]
         dense[where] += metric[k].astype(jnp.float32)
 
     for target, mine in ((keep, core), (send, 1 - core)):
@@ -259,74 +256,81 @@
     )(plan, slots, outs_of, metric)
 
 
-def middle_kernel(pairs, plan, mine, other, own, outward):
-    def total(k):
-        return (mine[k].astype(jnp.float32) + other[k].astype(jnp.float32)).astype(jnp.bfloat16)
-
-    shift = jnp.where(lax.axis_index("row") // 2 < pairs // 2, 0, 2)
-    base = plan[0]
+def pair_kernel(mine, came, near, far):
+    half = near.shape[0]
+    upper = (lax.axis_index("row") // 2 >= half).astype(jnp.int32)
+    for out, first in ((near, upper * half), (far, (1 - upper) * half)):
+        for k in range(half):
+            total = mine[first + k].astype(jnp.float32) + came[first + k].astype(jnp.float32)
+            out[k] = total.astype(jnp.bfloat16)
+
+
+def pair_section(mine, came):
+    pairs, _, span = mine.shape
+    return pl.pallas_call(
+        pair_kernel,
+        in_specs=[vmem(), vmem()],
+        out_specs=[vmem()] * 2,
+        out_shape=[jax.ShapeDtypeStruct((pairs // 2, BLOCK, span), jnp.bfloat16)] * 2,
+        compiler_params=params(),
+        cost_estimate=cost(mine.size, mine.size * 6),
+        name="pair_section",
+    )(mine, came)
+
+
+def line_kernel(*refs):
+    *parts, out = refs
+    for k in range(out.shape[0]):
+        total = parts[0][k].astype(jnp.float32)
+        for part in parts[1:]:
+            total = total + part[k].astype(jnp.float32)
+        out[k] = total.astype(jnp.bfloat16)
+
+
+def line_section(parts):
+    return pl.pallas_call(
+        line_kernel,
+        in_specs=[vmem()] * len(parts),
+        out_specs=vmem(),
+        out_shape=jax.ShapeDtypeStruct(parts[0].shape, jnp.bfloat16),
+        compiler_params=params(),
+        cost_estimate=cost(parts[0].size * len(parts), parts[0].size * 2 * len(parts)),
+        name="line_section",
+    )(*parts)
+
+
+def owned_kernel(half, plan, *refs):
+    *held, owned, away = refs
+    z = lax.axis_index("row") // 2
+    upper = (z >= half).astype(jnp.int32)
+    distance = jnp.where(z >= half, z - half, half - 1 - z)
     for k in range(2):
-        own[k] = total(base + k)
-    for k in range(pairs - 2):
-        outward[k] = total(shift + k)
-
-
-def middle_section(plan, mine, other):
-    pairs, _, span = mine.shape
-    return pl.pallas_call(
-        functools.partial(middle_kernel, pairs),
-        in_specs=[smem(), vmem(), vmem()],
+        block = plan[3] + k
+        block_upper = (block >= half).astype(jnp.int32)
+        wanted = distance + half * jnp.abs(block_upper - upper)
+        for d, blocks in enumerate(held):
+
+            @pl.when(wanted == d)
+            def _(blocks=blocks):
+                owned[k] = blocks[block - half * block_upper]
+
+    away[0] = owned[plan[0]]
+
+
+def owned_section(plan, held):
+    half, _, span = held[0].shape
+    return pl.pallas_call(
+        functools.partial(owned_kernel, half),
+        in_specs=[smem()] + [vmem()] * len(held),
         out_specs=[vmem(), vmem()],
         out_shape=[
             jax.ShapeDtypeStruct((2, BLOCK, span), jnp.bfloat16),
-            jax.ShapeDtypeStruct((pairs - 2, BLOCK, span), jnp.bfloat16),
+            jax.ShapeDtypeStruct((1, BLOCK, span), jnp.bfloat16),
         ],
         compiler_params=params(),
-        cost_estimate=cost(mine.size, mine.size * 6),
-        name="middle_section",
-    )(plan, mine, other)
-
-
-def outward_kernel(pairs, level, plan, own, came, own_out, rest):
-    z = lax.axis_index("row") // 2
-    lower = z < pairs // 2
-    distance = jnp.where(lower, pairs // 2 - 1 - z, z - pairs // 2)
-    here = distance == level
-    base = plan[0]
-
-    @pl.when(here)
-    def _():
-        for k in range(2):
-            own_out[k] = came[base + k]
-
-    @pl.when(jnp.logical_not(here))
-    def _():
-        for k in range(2):
-            own_out[k] = own[k]
-
-    if level == pairs // 2 - 1:
-        rest[0] = own_out[plan[1]]
-    else:
-        shift = jnp.where(lower, 0, 2)
-        for k in range(rest.shape[0]):
-            rest[k] = came[shift + k]
-
-
-def outward_section(plan, own, came, level, pairs):
-    span = own.shape[2]
-    last = level == pairs // 2 - 1
-    return pl.pallas_call(
-        functools.partial(outward_kernel, pairs, level),
-        in_specs=[smem(), vmem(), vmem()],
-        out_specs=[vmem(), vmem()],
-        out_shape=[
-            jax.ShapeDtypeStruct((2, BLOCK, span), jnp.bfloat16),
-            jax.ShapeDtypeStruct((1 if last else came.shape[0] - 2, BLOCK, span), jnp.bfloat16),
-        ],
-        compiler_params=params(),
-        cost_estimate=cost(0, own.size * 8),
-        name="outward_section",
-    )(plan, own, came)
+        cost_estimate=cost(0, held[0].size * 12),
+        name="owned_section",
+    )(plan, *held)
 
 
 def term_kernel(ys, keep, got, own, own_core, fix, fix_core, sent, kept):
@@ -366,17 +370,12 @@
     )(keep, got, own, own_core, fix, fix_core)
 
 
-def added(a, b):
-    return (a.astype(jnp.float32) + b.astype(jnp.float32)).astype(jnp.bfloat16)
-
-
 def per_device(
     coeff, tri_blocks, pair_aux, pair_ao, owner_slot, metric_blocks, pair_slot, pair_out
 ):
     rows = lax.axis_size("row")
     cols = lax.axis_size("col")
     pairs, ys = rows // 2, cols // 2
-    half = pairs // 2
 
     def on_line(moves):
         return [(2 * a + x, 2 * b + x) for a, b in moves for x in range(2)]
@@ -389,24 +388,33 @@
     keep, send = metric_section(plan, pair_slot, pair_out, metric_blocks, cols)
     got = lax.ppermute(send, "col", swap_core)
 
+    half = pairs // 2
+    near_moves = [[(half - 1 - e, half - 1), (half + e, half)] for e in range(1, half)]
+    far_moves = [[(half - 1 - e, half), (half + e, half - 1)] for e in range(half)]
+    inward = [on_line(m) for m in near_moves], [on_line(m) for m in far_moves]
+    beyond = pairs - (pairs - half) // 2 - half
+    outward = [on_line([(b, a) for a, b in m]) for m in near_moves] + [
+        on_line([(half - 1, half + e), (half, half - 1 - e)]) for e in range(beyond)
+    ]
+    around = [
+        [(2 * y + k, 2 * ((y + d) % ys) + k) for y in range(ys) for k in range(2)] for d in range(1, ys)
+    ]
+
     finished = []
     for piece in range(NUW):
-        total = added(made[2 * piece], lax.ppermute(made[2 * piece + 1], "row", swap_pair))
-        for a in range(half - 1):
-            inward = on_line([(a, a + 1), (pairs - 1 - a, pairs - 2 - a)])
-            total = added(total, lax.ppermute(total, "row", inward))
-        other = lax.ppermute(total, "row", on_line([(half - 1, half), (half, half - 1)]))
-        own, rest = middle_section(plan, total, other)
-        for level in range(1, half):
-            outward = on_line([(half - level, half - 1 - level), (half - 1 + level, half + level)])
-            own, rest = outward_section(plan, own, lax.ppermute(rest, "row", outward), level, pairs)
-        fix = lax.ppermute(rest, "row", swap_pair)
+        came = lax.ppermute(made[2 * piece + 1], "row", swap_pair)
+        near, far = pair_section(made[2 * piece], came)
+        parts = [lax.ppermute(far, "row", moves) for moves in inward[1]]
+        parts += [lax.ppermute(near, "row", moves) for moves in inward[0]]
+        host = line_section([near, *parts])
+        held = [host] + [lax.ppermute(host, "row", moves) for moves in outward]
+        own, away = owned_section(plan, held)
+        fix = lax.ppermute(away, "row", swap_pair)
         own_core = lax.ppermute(own, "col", swap_core)
         fix_core = lax.ppermute(fix, "col", swap_core)
         sent, kept = term_section(keep, got, own, own_core, fix, fix_core)
         for d in range(1, ys):
-            around = [(2 * y + k, 2 * ((y + d) % ys) + k) for y in range(ys) for k in range(2)]
-            kept = kept + lax.ppermute(sent[d - 1], "col", around).astype(jnp.float32)
+            kept = kept + lax.ppermute(sent[d - 1], "col", around[d - 1]).astype(jnp.float32)
         finished.append(kept.astype(jnp.bfloat16))
     return jnp.concatenate(finished, axis=1)
 

time: 89.2 us -> 82.4 us (0.924)
  waiting for transfers between devices: 49.6 us -> 38.4 us
  starting transfers between devices: 21.5 us -> 27.2 us
    ppermute x12 -> x16, waiting for transfers between devices: 48.3 us -> 37.1 us  [the longest x2 13.1 us: per_device(): came = lax.ppermute(made[2 * piece + 1], 'row', swap_pair)]
    ppermute x12 -> x16, starting transfers between devices: 21.3 us -> 27.1 us  [the longest x2 7.8 us: per_device(): parts += [lax.ppermute(near, 'row', moves) for moves in inward[0]]]
    pallas_call x4 -> x6, Pallas kernels: 2.52 us -> 1.76 us  [the longest x2 1.26 us: owned_section(): pl.pallas_call(functools.partial(owned_kernel, half), in_specs=[smem()] +...]
  transfers between devices with their start and end apart: 17 -> 21, of which waited for: 10 -> 10; matrix products, arithmetic and copies ran while one was open for 1% -> 0% of each run, Pallas kernels for 8% -> 7%
where the time goes in v3:
time: 82.4 us; the launch traced here: 82.1 us
  waiting for transfers between devices  38.4 us (47%)
  starting transfers between devices  27.2 us (33%)
  Pallas kernels  13.6 us (17%)
  local copies, waits for them, and re-layouts  1.62 us (2%)
  other arithmetic  1.01 us (1%)
    ppermute x2, waiting for transfers between devices, per_device(): came = lax.ppermute(made[2 * piece + 1], 'row', swap_pair)  13.1 us
    ppermute x4, waiting for transfers between devices, per_device(): held = [host] + [lax.ppermute(host, 'row', moves) for moves in outward]  7.97 us
    ppermute x2, waiting for transfers between devices, per_device(): lax.ppermute(sent[d - 1], 'col', around[d - 1]).astype(jnp.float32)  7.93 us
    ppermute x2, starting transfers between devices, per_device(): parts += [lax.ppermute(near, 'row', moves) for moves in inward[0]]  7.8 us
    pallas_call x1, Pallas kernels, first_section(): pl.pallas_call(functools.partial(first_kernel, rows, table, group), in_sp...  7.63 us
    ppermute x4, starting transfers between devices, per_device(): parts = [lax.ppermute(far, 'row', moves) for moves in inward[1]]  5.97 us
    ppermute x2, waiting for transfers between devices, per_device(): fix = lax.ppermute(away, 'row', swap_pair)  4.77 us
    ppermute x4, starting transfers between devices, per_device(): held = [host] + [lax.ppermute(host, 'row', moves) for moves in outward]  3.94 us
  transfers between devices with their start and end apart: 21, of which 10 were waited for; matrix products, arithmetic and copies ran while one was open for 0% of the time, Pallas kernels for 7%

profile of v3, /device:TPU:0, one launch (start us, length us, event | category | flops | bytes accessed | tf_op | source)
XLA Modules:
  0.0 82.1 jit_solution(421672736340049101)
XLA Ops:
  0.0 7.6 %first_section.1 = (bf16[4,128,512]{2,1,0:T(8,128)(2,1)}, bf16[4,128,512]{2,1,0:T(8,128)(2,1)}, s32[4]{0:T(128)}, bf16[8,128,1024]{2,1,0:T(8,128)(2,1)}) custom-call(s32[160]{0:T(256)} %aux_in.1, s32[160]{0:T(256)} %ao_in.1, s32[1,8]{1,0:T(1,128)} %owner_in.1, bf16[160,256,128]{2,1,0:T(8,128)(2,1)} %tiles_in.1, bf16[1024,512]{1,0:T(8,128)(2,1)} %coeff.1), custom_call_target="tpu_custom_call" | custom-call | flops 1073741824 | bytes 11534336 | tf_op jit(solution)/shard_map/first_section/pallas_call | solution.py:163
  7.6 0.0 copy-start.2
  7.7 3.0 %collective-permute-start.1 = (bf16[4,128,512]{2,1,0:T(8,128)(2,1)}, bf16[4,128,512]{2,1,0:T(8,128)(2,1)S(1)}, u32[]{:S(2)}, u32[]{:S(2)}) collective-permute-start(bf16[4,128,512]{2,1,0:T(8,128)(2,1)} %get-tuple-element.29), channel_id=1, source_target_pairs={{0,4},{4,0},{8,12},{12,8},{16,20},{20,16},{24,28},{28,24},{1,5},{5... | collective-permute-start | bytes 1572872 | tf_op jit(solution)/shard_map/ppermute | solution.py:405
  10.7 1.6 %copy-done.6 = bf16[8,128,1024]{2,1,0:T(8,128)(2,1)S(1)} copy-done((bf16[8,128,1024]{2,1,0:T(8,128)(2,1)S(1)}, bf16[8,128,1024]{2,1,0:T(8,128)(2,1)}, u32[]{:S(2)}) %copy-start.6) | copy-done | bytes 2097176
  12.3 1.2 %later_section.1 = (bf16[4,128,512]{2,1,0:T(8,128)(2,1)S(1)}, bf16[4,128,512]{2,1,0:T(8,128)(2,1)S(1)}) custom-call(bf16[8,128,1024]{2,1,0:T(8,128)(2,1)S(1)} %copy-done.6, bf16[1024,512]{1,0:T(8,128)(2,1)S(1)} %copy-done.1), custom_call_target="tpu_custom_call" | custom-call | flops 1073741824 | bytes 4194304 | tf_op jit(solution)/shard_map/later_section/pallas_call | solution.py:210
  13.5 0.0 copy-start
  13.5 0.0 copy-start.4
  13.5 0.0 copy-start.5
  13.6 0.1 collective-permute-start.11
  13.7 9.9 %collective-permute-done.1.came = bf16[4,128,512]{2,1,0:T(8,128)(2,1)S(1)} collective-permute-done((bf16[4,128,512]{2,1,0:T(8,128)(2,1)}, bf16[4,128,512]{2,1,0:T(8,128)(2,1)S(1)}, u32[]{:S(2)}, u32[]{:S(2)}) %collective-permute-start.1) | collective-permute-done | bytes 524320 | tf_op jit(solution)/shard_map/ppermute | solution.py:405
  23.6 0.0 copy-done.2
  23.6 0.1 pair_section.2
  23.8 4.1 %collective-permute-start.4 = (bf16[2,128,512]{2,1,0:T(8,128)(2,1)S(1)}, bf16[2,128,512]{2,1,0:T(8,128)(2,1)S(1)}, u32[]{:S(2)}, u32[]{:S(2)}) collective-permute-start(bf16[2,128,512]{2,1,0:T(8,128)(2,1)S(1)} %get-tuple-element.30.refs_0_), channel_id=1, source_target_pairs={{0,8},{4,12},{24,16},{28,20},{1,9},{5,13},{25,17},{29,21},{2,10},{... | collective-permute-start | bytes 786440 | tf_op jit(solution)/shard_map/ppermute | solution.py:408
  27.8 2.3 %collective-permute-start.3 = (bf16[2,128,512]{2,1,0:T(8,128)(2,1)S(1)}, bf16[2,128,512]{2,1,0:T(8,128)(2,1)S(1)}, u32[]{:S(2)}, u32[]{:S(2)}) collective-permute-start(bf16[2,128,512]{2,1,0:T(8,128)(2,1)S(1)} %get-tuple-element.31), channel_id=1, source_target_pairs={{0,16},{4,20},{24,8},{28,12},{1,17},{5,21},{25,9},{29,13},{2,18},{... | collective-permute-start | bytes 786440 | tf_op jit(solution)/shard_map/ppermute | solution.py:407
  30.1 0.7 collective-permute-start.2
  30.8 3.2 %collective-permute-done.11.came = bf16[4,128,512]{2,1,0:T(8,128)(2,1)S(1)} collective-permute-done((bf16[4,128,512]{2,1,0:T(8,128)(2,1)S(1)}, bf16[4,128,512]{2,1,0:T(8,128)(2,1)S(1)}, u32[]{:S(2)}, u32[]{:S(2)}) %collective-permute-start.11) | collective-permute-done | bytes 524320 | tf_op jit(solution)/shard_map/ppermute | solution.py:405
  34.0 0.1 pair_section.3
  34.2 3.7 %collective-permute-start.14 = (bf16[2,128,512]{2,1,0:T(8,128)(2,1)S(1)}, bf16[2,128,512]{2,1,0:T(8,128)(2,1)S(1)}, u32[]{:S(2)}, u32[]{:S(2)}) collective-permute-start(bf16[2,128,512]{2,1,0:T(8,128)(2,1)S(1)} %get-tuple-element.39.refs_0_), channel_id=1, source_target_pairs={{0,8},{4,12},{24,16},{28,20},{1,9},{5,13},{25,17},{29,21},{2,10},{... | collective-permute-start | bytes 786440 | tf_op jit(solution)/shard_map/ppermute | solution.py:408
  37.9 2.3 %collective-permute-start.13 = (bf16[2,128,512]{2,1,0:T(8,128)(2,1)S(1)}, bf16[2,128,512]{2,1,0:T(8,128)(2,1)S(1)}, u32[]{:S(2)}, u32[]{:S(2)}) collective-permute-start(bf16[2,128,512]{2,1,0:T(8,128)(2,1)S(1)} %get-tuple-element.40), channel_id=1, source_target_pairs={{0,16},{4,20},{24,8},{28,12},{1,17},{5,21},{25,9},{29,13},{2,18},{... | collective-permute-start | bytes 786440 | tf_op jit(solution)/shard_map/ppermute | solution.py:407
  40.2 0.0 collective-permute-done.4.refs_3_
  40.2 0.7 collective-permute-start.12
  40.9 0.0 collective-permute-done.3.refs_2_
  40.9 0.0 collective-permute-done.2.refs_1_
  40.9 0.1 line_section.2.refs_0_
  41.1 0.7 collective-permute-start.6
  41.8 1.3 %collective-permute-start.5 = (bf16[2,128,512]{2,1,0:T(8,128)(2,1)S(1)}, bf16[2,128,512]{2,1,0:T(8,128)(2,1)S(1)}, u32[]{:S(2)}, u32[]{:S(2)}) collective-permute-start(bf16[2,128,512]{2,1,0:T(8,128)(2,1)S(1)} %line_section.2.refs_0_), channel_id=1, source_target_pairs={{8,0},{12,4},{16,24},{20,28},{9,1},{13,5},{17,25},{21,29},{10,2},{... | collective-permute-start | bytes 786440 | tf_op jit(solution)/shard_map/ppermute | solution.py:410
  43.1 0.0 copy-done
  43.1 0.0 copy-done.3
  43.1 1.8 %metric_section.1 = (bf16[2,256,384]{2,1,0:T(8,128)(2,1)S(1)}, bf16[2,256,384]{2,1,0:T(8,128)(2,1)S(1)}) custom-call(s32[4]{0:T(128)S(1)} %copy-done.3, s32[64]{0:T(128)S(1)} %copy-done.4, s32[64]{0:T(128)S(1)} %copy-done.5, bf16[64,128,128]{2,1,0:T(8,128)(2,1)S(1)} %copy-done), custom_call_target="tpu_custom_call" | custom-call | bytes 3697152 | tf_op jit(solution)/shard_map/metric_section/pallas_call | solution.py:247
  44.9 0.0 collective-permute-done.14.refs_3_
  44.9 0.1 collective-permute-start
  45.0 3.2 %collective-permute-done.13.refs_2_ = bf16[2,128,512]{2,1,0:T(8,128)(2,1)S(1)} collective-permute-done((bf16[2,128,512]{2,1,0:T(8,128)(2,1)S(1)}, bf16[2,128,512]{2,1,0:T(8,128)(2,1)S(1)}, u32[]{:S(2)}, u32[]{:S(2)}) %collective-permute-start.13) | collective-permute-done | bytes 262176 | tf_op jit(solution)/shard_map/ppermute | solution.py:407
  48.2 0.0 collective-permute-done.12.refs_1_
  48.2 0.1 line_section.3.refs_0_
  48.4 0.7 collective-permute-start.16
  49.1 1.3 %collective-permute-start.15 = (bf16[2,128,512]{2,1,0:T(8,128)(2,1)S(1)}, bf16[2,128,512]{2,1,0:T(8,128)(2,1)S(1)}, u32[]{:S(2)}, u32[]{:S(2)}) collective-permute-start(bf16[2,128,512]{2,1,0:T(8,128)(2,1)S(1)} %line_section.3.refs_0_), channel_id=1, source_target_pairs={{8,0},{12,4},{16,24},{20,28},{9,1},{13,5},{17,25},{21,29},{10,2},{... | collective-permute-start | bytes 786440 | tf_op jit(solution)/shard_map/ppermute | solution.py:410
  50.4 0.0 collective-permute-done.6.refs_2_
  50.4 1.4 %collective-permute-done.5.refs_1_ = bf16[2,128,512]{2,1,0:T(8,128)(2,1)S(1)} collective-permute-done((bf16[2,128,512]{2,1,0:T(8,128)(2,1)S(1)}, bf16[2,128,512]{2,1,0:T(8,128)(2,1)S(1)}, u32[]{:S(2)}, u32[]{:S(2)}) %collective-permute-start.5) | collective-permute-done | bytes 262176 | tf_op jit(solution)/shard_map/ppermute | solution.py:410
  51.8 0.6 owned_section.2
  52.4 1.6 %collective-permute-start.8 = (bf16[1,128,512]{2,1,0:T(8,128)(2,1)S(1)}, bf16[1,128,512]{2,1,0:T(8,128)(2,1)S(1)}, u32[]{:S(2)}, u32[]{:S(2)}) collective-permute-start(bf16[1,128,512]{2,1,0:T(8,128)(2,1)S(1)} %get-tuple-element.33), channel_id=1, source_target_pairs={{0,4},{4,0},{8,12},{12,8},{16,20},{20,16},{24,28},{28,24},{1,5},{5... | collective-permute-start | bytes 393224 | tf_op jit(solution)/shard_map/ppermute | solution.py:412
  53.9 0.0 collective-permute-start.7
  53.9 3.5 %collective-permute-done.8.fix = bf16[1,128,512]{2,1,0:T(8,128)(2,1)S(1)} collective-permute-done((bf16[1,128,512]{2,1,0:T(8,128)(2,1)S(1)}, bf16[1,128,512]{2,1,0:T(8,128)(2,1)S(1)}, u32[]{:S(2)}, u32[]{:S(2)}) %collective-permute-start.8) | collective-permute-done | bytes 131104 | tf_op jit(solution)/shard_map/ppermute | solution.py:412
  57.4 0.0 collective-permute-start.9
  57.4 0.0 collective-permute-done.16.refs_2_
  57.4 6.6 %collective-permute-done.15.refs_1_ = bf16[2,128,512]{2,1,0:T(8,128)(2,1)S(1)} collective-permute-done((bf16[2,128,512]{2,1,0:T(8,128)(2,1)S(1)}, bf16[2,128,512]{2,1,0:T(8,128)(2,1)S(1)}, u32[]{:S(2)}, u32[]{:S(2)}) %collective-permute-start.15) | collective-permute-done | bytes 262176 | tf_op jit(solution)/shard_map/ppermute | solution.py:410
  64.0 0.6 owned_section.3
  64.6 1.6 %collective-permute-start.18 = (bf16[1,128,512]{2,1,0:T(8,128)(2,1)S(1)}, bf16[1,128,512]{2,1,0:T(8,128)(2,1)S(1)}, u32[]{:S(2)}, u32[]{:S(2)}) collective-permute-start(bf16[1,128,512]{2,1,0:T(8,128)(2,1)S(1)} %get-tuple-element.42), channel_id=1, source_target_pairs={{0,4},{4,0},{8,12},{12,8},{16,20},{20,16},{24,28},{28,24},{1,5},{5... | collective-permute-start | bytes 393224 | tf_op jit(solution)/shard_map/ppermute | solution.py:412
  66.2 0.0 collective-permute-start.17
  66.2 0.0 collective-permute-done.got
  66.2 0.0 collective-permute-done.9.fix_core
  66.2 0.0 collective-permute-done.7.own_core
  66.2 0.6 term_section.2
  66.8 1.6 %collective-permute-start.10 = (bf16[256,512]{1,0:T(8,128)(2,1)S(1)}, bf16[256,512]{1,0:T(8,128)(2,1)S(1)}, u32[]{:S(2)}, u32[]{:S(2)}) collective-permute-start(bf16[256,512]{1,0:T(8,128)(2,1)S(1)} %bitcast.2), channel_id=1, source_target_pairs={{0,2},{1,3},{2,0},{3,1},{4,6},{5,7},{6,4},{7,5},{8,10},{9,11},{10,... | collective-permute-start | bytes 786440 | tf_op jit(solution)/shard_map/ppermute | solution.py:417
  68.4 1.3 %collective-permute-done.18.fix = bf16[1,128,512]{2,1,0:T(8,128)(2,1)S(1)} collective-permute-done((bf16[1,128,512]{2,1,0:T(8,128)(2,1)S(1)}, bf16[1,128,512]{2,1,0:T(8,128)(2,1)S(1)}, u32[]{:S(2)}, u32[]{:S(2)}) %collective-permute-start.18) | collective-permute-done | bytes 131104 | tf_op jit(solution)/shard_map/ppermute | solution.py:412
  69.7 0.0 collective-permute-start.19
  69.7 1.3 %collective-permute-done.19.fix_core = bf16[1,128,512]{2,1,0:T(8,128)(2,1)S(1)} collective-permute-done((bf16[1,128,512]{2,1,0:T(8,128)(2,1)S(1)}, bf16[1,128,512]{2,1,0:T(8,128)(2,1)S(1)}, u32[]{:S(2)}, u32[]{:S(2)}) %collective-permute-start.19) | collective-permute-done | bytes 131104 | tf_op jit(solution)/shard_map/ppermute | solution.py:414
  71.0 0.0 collective-permute-done.17.own_core
  71.0 0.6 term_section.3
  71.6 1.6 %collective-permute-start.20 = (bf16[256,512]{1,0:T(8,128)(2,1)S(1)}, bf16[256,512]{1,0:T(8,128)(2,1)S(1)}, u32[]{:S(2)}, u32[]{:S(2)}) collective-permute-start(bf16[256,512]{1,0:T(8,128)(2,1)S(1)} %bitcast.3), channel_id=1, source_target_pairs={{0,2},{1,3},{2,0},{3,1},{4,6},{5,7},{6,4},{7,5},{8,10},{9,11},{10,... | collective-permute-start | bytes 786440 | tf_op jit(solution)/shard_map/ppermute | solution.py:417
  73.2 2.8 %collective-permute-done.10 = bf16[256,512]{1,0:T(8,128)(2,1)S(1)} collective-permute-done((bf16[256,512]{1,0:T(8,128)(2,1)S(1)}, bf16[256,512]{1,0:T(8,128)(2,1)S(1)}, u32[]{:S(2)}, u32[]{:S(2)}) %collective-permute-start.10) | collective-permute-done | bytes 262176 | tf_op jit(solution)/shard_map/ppermute | solution.py:417
  76.0 0.1 add_convert_fusion.1
  76.0 5.2 %collective-permute-done.20 = bf16[256,512]{1,0:T(8,128)(2,1)S(1)} collective-permute-done((bf16[256,512]{1,0:T(8,128)(2,1)S(1)}, bf16[256,512]{1,0:T(8,128)(2,1)S(1)}, u32[]{:S(2)}, u32[]{:S(2)}) %collective-permute-start.20) | collective-permute-done | bytes 262176 | tf_op jit(solution)/shard_map/ppermute | solution.py:417
  81.2 0.1 add_convert_fusion
  81.3 0.9 %pad_maximum_fusion = bf16[256,1024]{1,0:T(8,128)(2,1)} fusion(bf16[256,512]{1,0:T(8,128)(2,1)S(1)} %add_convert_fusion, bf16[256,512]{1,0:T(8,128)(2,1)S(1)} %add_convert_fusion.1), kind=kLoop, calls=%fused_computation | loop fusion | flops 1048576 | bytes 1048576 | tf_op jit(solution)/shard_map/concatenate | solution.py:419
  (6 shorter events, 0.0 us)
Async XLA Ops:
  0.0 10.7 %copy-start.1 = (bf16[1024,512]{1,0:T(8,128)(2,1)S(1)}, bf16[1024,512]{1,0:T(8,128)(2,1)}, u32[]{:S(2)}) copy-start(bf16[1024,512]{1,0:T(8,128)(2,1)} %coeff.1) | copy-start | bytes 3145732
  7.6 16.0 %copy-start.2 = (bf16[4,128,512]{2,1,0:T(8,128)(2,1)S(1)}, bf16[4,128,512]{2,1,0:T(8,128)(2,1)}, u32[]{:S(2)}) copy-start(bf16[4,128,512]{2,1,0:T(8,128)(2,1)} %get-tuple-element.28.mine) | copy-start | bytes 1572868
  7.7 16.0 %collective-permute-start.1 = (bf16[4,128,512]{2,1,0:T(8,128)(2,1)}, bf16[4,128,512]{2,1,0:T(8,128)(2,1)S(1)}, u32[]{:S(2)}, u32[]{:S(2)}) collective-permute-start(bf16[4,128,512]{2,1,0:T(8,128)(2,1)} %get-tuple-element.29), channel_id=1, source_target_pairs={{0,4},{4,0},{8,12},{12,8},{16,20},{20,16},{24,28},{28,24},{1,5},{5... | collective-permute-start | bytes 1572872 | tf_op jit(solution)/shard_map/ppermute | solution.py:405
  10.7 1.6 %copy-start.6 = (bf16[8,128,1024]{2,1,0:T(8,128)(2,1)S(1)}, bf16[8,128,1024]{2,1,0:T(8,128)(2,1)}, u32[]{:S(2)}) copy-start(bf16[8,128,1024]{2,1,0:T(8,128)(2,1)} %get-tuple-element.36.left) | copy-start | bytes 6291460
  13.5 29.6 %copy-start = (bf16[64,128,128]{2,1,0:T(8,128)(2,1)S(1)}, bf16[64,128,128]{2,1,0:T(8,128)(2,1)}, u32[]{:S(2)}) copy-start(bf16[64,128,128]{2,1,0:T(8,128)(2,1)} %metric.1) | copy-start | bytes 6291460
  13.5 29.6 %copy-start.3 = (s32[4]{0:T(128)S(1)}, s32[4]{0:T(128)}, u32[]{:S(2)}) copy-start(s32[4]{0:T(128)} %get-tuple-element.25.plan) | copy-start | bytes 52
  13.5 29.6 %copy-start.4 = (s32[64]{0:T(128)S(1)}, s32[64]{0:T(128)}, u32[]{:S(2)}) copy-start(s32[64]{0:T(128)} %slots.1) | copy-start | bytes 772
  13.5 29.6 %copy-start.5 = (s32[64]{0:T(128)S(1)}, s32[64]{0:T(128)}, u32[]{:S(2)}) copy-start(s32[64]{0:T(128)} %outs_of.1) | copy-start | bytes 772
  13.6 20.5 %collective-permute-start.11 = (bf16[4,128,512]{2,1,0:T(8,128)(2,1)S(1)}, bf16[4,128,512]{2,1,0:T(8,128)(2,1)S(1)}, u32[]{:S(2)}, u32[]{:S(2)}) collective-permute-start(bf16[4,128,512]{2,1,0:T(8,128)(2,1)S(1)} %get-tuple-element.38), channel_id=1, source_target_pairs={{0,4},{4,0},{8,12},{12,8},{16,20},{20,16},{24,28},{28,24},{1,5},{5... | collective-permute-start | bytes 1572872 | tf_op jit(solution)/shard_map/ppermute | solution.py:405
  23.8 16.5 %collective-permute-start.4 = (bf16[2,128,512]{2,1,0:T(8,128)(2,1)S(1)}, bf16[2,128,512]{2,1,0:T(8,128)(2,1)S(1)}, u32[]{:S(2)}, u32[]{:S(2)}) collective-permute-start(bf16[2,128,512]{2,1,0:T(8,128)(2,1)S(1)} %get-tuple-element.30.refs_0_), channel_id=1, source_target_pairs={{0,8},{4,12},{24,16},{28,20},{1,9},{5,13},{25,17},{29,21},{2,10},{... | collective-permute-start | bytes 786440 | tf_op jit(solution)/shard_map/ppermute | solution.py:408
  27.8 13.1 %collective-permute-start.3 = (bf16[2,128,512]{2,1,0:T(8,128)(2,1)S(1)}, bf16[2,128,512]{2,1,0:T(8,128)(2,1)S(1)}, u32[]{:S(2)}, u32[]{:S(2)}) collective-permute-start(bf16[2,128,512]{2,1,0:T(8,128)(2,1)S(1)} %get-tuple-element.31), channel_id=1, source_target_pairs={{0,16},{4,20},{24,8},{28,12},{1,17},{5,21},{25,9},{29,13},{2,18},{... | collective-permute-start | bytes 786440 | tf_op jit(solution)/shard_map/ppermute | solution.py:407
  30.1 10.8 %collective-permute-start.2 = (bf16[2,128,512]{2,1,0:T(8,128)(2,1)S(1)}, bf16[2,128,512]{2,1,0:T(8,128)(2,1)S(1)}, u32[]{:S(2)}, u32[]{:S(2)}) collective-permute-start(bf16[2,128,512]{2,1,0:T(8,128)(2,1)S(1)} %get-tuple-element.31), channel_id=1, source_target_pairs={{8,16},{12,20},{16,8},{20,12},{9,17},{13,21},{17,9},{21,13},{10,18... | collective-permute-start | bytes 786440 | tf_op jit(solution)/shard_map/ppermute | solution.py:407
  34.2 10.8 %collective-permute-start.14 = (bf16[2,128,512]{2,1,0:T(8,128)(2,1)S(1)}, bf16[2,128,512]{2,1,0:T(8,128)(2,1)S(1)}, u32[]{:S(2)}, u32[]{:S(2)}) collective-permute-start(bf16[2,128,512]{2,1,0:T(8,128)(2,1)S(1)} %get-tuple-element.39.refs_0_), channel_id=1, source_target_pairs={{0,8},{4,12},{24,16},{28,20},{1,9},{5,13},{25,17},{29,21},{2,10},{... | collective-permute-start | bytes 786440 | tf_op jit(solution)/shard_map/ppermute | solution.py:408
  37.9 10.3 %collective-permute-start.13 = (bf16[2,128,512]{2,1,0:T(8,128)(2,1)S(1)}, bf16[2,128,512]{2,1,0:T(8,128)(2,1)S(1)}, u32[]{:S(2)}, u32[]{:S(2)}) collective-permute-start(bf16[2,128,512]{2,1,0:T(8,128)(2,1)S(1)} %get-tuple-element.40), channel_id=1, source_target_pairs={{0,16},{4,20},{24,8},{28,12},{1,17},{5,21},{25,9},{29,13},{2,18},{... | collective-permute-start | bytes 786440 | tf_op jit(solution)/shard_map/ppermute | solution.py:407
  40.2 8.0 %collective-permute-start.12 = (bf16[2,128,512]{2,1,0:T(8,128)(2,1)S(1)}, bf16[2,128,512]{2,1,0:T(8,128)(2,1)S(1)}, u32[]{:S(2)}, u32[]{:S(2)}) collective-permute-start(bf16[2,128,512]{2,1,0:T(8,128)(2,1)S(1)} %get-tuple-element.40), channel_id=1, source_target_pairs={{8,16},{12,20},{16,8},{20,12},{9,17},{13,21},{17,9},{21,13},{10,18... | collective-permute-start | bytes 786440 | tf_op jit(solution)/shard_map/ppermute | solution.py:407
  41.1 9.3 %collective-permute-start.6 = (bf16[2,128,512]{2,1,0:T(8,128)(2,1)S(1)}, bf16[2,128,512]{2,1,0:T(8,128)(2,1)S(1)}, u32[]{:S(2)}, u32[]{:S(2)}) collective-permute-start(bf16[2,128,512]{2,1,0:T(8,128)(2,1)S(1)} %line_section.2.refs_0_), channel_id=1, source_target_pairs={{8,16},{12,20},{16,8},{20,12},{9,17},{13,21},{17,9},{21,13},{10,18... | collective-permute-start | bytes 786440 | tf_op jit(solution)/shard_map/ppermute | solution.py:410
  41.8 10.0 %collective-permute-start.5 = (bf16[2,128,512]{2,1,0:T(8,128)(2,1)S(1)}, bf16[2,128,512]{2,1,0:T(8,128)(2,1)S(1)}, u32[]{:S(2)}, u32[]{:S(2)}) collective-permute-start(bf16[2,128,512]{2,1,0:T(8,128)(2,1)S(1)} %line_section.2.refs_0_), channel_id=1, source_target_pairs={{8,0},{12,4},{16,24},{20,28},{9,1},{13,5},{17,25},{21,29},{10,2},{... | collective-permute-start | bytes 786440 | tf_op jit(solution)/shard_map/ppermute | solution.py:410
  44.9 21.3 %collective-permute-start = (bf16[2,256,384]{2,1,0:T(8,128)(2,1)S(1)}, bf16[2,256,384]{2,1,0:T(8,128)(2,1)S(1)}, u32[]{:S(2)}, u32[]{:S(2)}) collective-permute-start(bf16[2,256,384]{2,1,0:T(8,128)(2,1)S(1)} %get-tuple-element.27), channel_id=1, source_target_pairs={{0,1},{1,0},{2,3},{3,2},{4,5},{5,4},{6,7},{7,6},{8,9},{9,8},{10,11... | collective-permute-start | bytes 1179656 | tf_op jit(solution)/shard_map/ppermute | solution.py:389
  48.4 9.1 %collective-permute-start.16 = (bf16[2,128,512]{2,1,0:T(8,128)(2,1)S(1)}, bf16[2,128,512]{2,1,0:T(8,128)(2,1)S(1)}, u32[]{:S(2)}, u32[]{:S(2)}) collective-permute-start(bf16[2,128,512]{2,1,0:T(8,128)(2,1)S(1)} %line_section.3.refs_0_), channel_id=1, source_target_pairs={{8,16},{12,20},{16,8},{20,12},{9,17},{13,21},{17,9},{21,13},{10,18... | collective-permute-start | bytes 786440 | tf_op jit(solution)/shard_map/ppermute | solution.py:410
  49.1 15.0 %collective-permute-start.15 = (bf16[2,128,512]{2,1,0:T(8,128)(2,1)S(1)}, bf16[2,128,512]{2,1,0:T(8,128)(2,1)S(1)}, u32[]{:S(2)}, u32[]{:S(2)}) collective-permute-start(bf16[2,128,512]{2,1,0:T(8,128)(2,1)S(1)} %line_section.3.refs_0_), channel_id=1, source_target_pairs={{8,0},{12,4},{16,24},{20,28},{9,1},{13,5},{17,25},{21,29},{10,2},{... | collective-permute-start | bytes 786440 | tf_op jit(solution)/shard_map/ppermute | solution.py:410
  52.4 5.0 %collective-permute-start.8 = (bf16[1,128,512]{2,1,0:T(8,128)(2,1)S(1)}, bf16[1,128,512]{2,1,0:T(8,128)(2,1)S(1)}, u32[]{:S(2)}, u32[]{:S(2)}) collective-permute-start(bf16[1,128,512]{2,1,0:T(8,128)(2,1)S(1)} %get-tuple-element.33), channel_id=1, source_target_pairs={{0,4},{4,0},{8,12},{12,8},{16,20},{20,16},{24,28},{28,24},{1,5},{5... | collective-permute-start | bytes 393224 | tf_op jit(solution)/shard_map/ppermute | solution.py:412
  53.9 12.3 %collective-permute-start.7 = (bf16[2,128,512]{2,1,0:T(8,128)(2,1)S(1)}, bf16[2,128,512]{2,1,0:T(8,128)(2,1)S(1)}, u32[]{:S(2)}, u32[]{:S(2)}) collective-permute-start(bf16[2,128,512]{2,1,0:T(8,128)(2,1)S(1)} %get-tuple-element.32.own), channel_id=1, source_target_pairs={{0,1},{1,0},{2,3},{3,2},{4,5},{5,4},{6,7},{7,6},{8,9},{9,8},{10,11... | collective-permute-start | bytes 786440 | tf_op jit(solution)/shard_map/ppermute | solution.py:413
  57.4 8.8 %collective-permute-start.9 = (bf16[1,128,512]{2,1,0:T(8,128)(2,1)S(1)}, bf16[1,128,512]{2,1,0:T(8,128)(2,1)S(1)}, u32[]{:S(2)}, u32[]{:S(2)}) collective-permute-start(bf16[1,128,512]{2,1,0:T(8,128)(2,1)S(1)} %collective-permute-done.8.fix), channel_id=1, source_target_pairs={{0,1},{1,0},{2,3},{3,2},{4,5},{5,4},{6,7},{7,6},{8,9},{9,8},{10,11... | collective-permute-start | bytes 393224 | tf_op jit(solution)/shard_map/ppermute | solution.py:414
  64.6 5.0 %collective-permute-start.18 = (bf16[1,128,512]{2,1,0:T(8,128)(2,1)S(1)}, bf16[1,128,512]{2,1,0:T(8,128)(2,1)S(1)}, u32[]{:S(2)}, u32[]{:S(2)}) collective-permute-start(bf16[1,128,512]{2,1,0:T(8,128)(2,1)S(1)} %get-tuple-element.42), channel_id=1, source_target_pairs={{0,4},{4,0},{8,12},{12,8},{16,20},{20,16},{24,28},{28,24},{1,5},{5... | collective-permute-start | bytes 393224 | tf_op jit(solution)/shard_map/ppermute | solution.py:412
  66.2 4.8 %collective-permute-start.17 = (bf16[2,128,512]{2,1,0:T(8,128)(2,1)S(1)}, bf16[2,128,512]{2,1,0:T(8,128)(2,1)S(1)}, u32[]{:S(2)}, u32[]{:S(2)}) collective-permute-start(bf16[2,128,512]{2,1,0:T(8,128)(2,1)S(1)} %get-tuple-element.41.own), channel_id=1, source_target_pairs={{0,1},{1,0},{2,3},{3,2},{4,5},{5,4},{6,7},{7,6},{8,9},{9,8},{10,11... | collective-permute-start | bytes 786440 | tf_op jit(solution)/shard_map/ppermute | solution.py:413
  66.8 9.2 %collective-permute-start.10 = (bf16[256,512]{1,0:T(8,128)(2,1)S(1)}, bf16[256,512]{1,0:T(8,128)(2,1)S(1)}, u32[]{:S(2)}, u32[]{:S(2)}) collective-permute-start(bf16[256,512]{1,0:T(8,128)(2,1)S(1)} %bitcast.2), channel_id=1, source_target_pairs={{0,2},{1,3},{2,0},{3,1},{4,6},{5,7},{6,4},{7,5},{8,10},{9,11},{10,... | collective-permute-start | bytes 786440 | tf_op jit(solution)/shard_map/ppermute | solution.py:417
  69.7 1.3 %collective-permute-start.19 = (bf16[1,128,512]{2,1,0:T(8,128)(2,1)S(1)}, bf16[1,128,512]{2,1,0:T(8,128)(2,1)S(1)}, u32[]{:S(2)}, u32[]{:S(2)}) collective-permute-start(bf16[1,128,512]{2,1,0:T(8,128)(2,1)S(1)} %collective-permute-done.18.fix), channel_id=1, source_target_pairs={{0,1},{1,0},{2,3},{3,2},{4,5},{5,4},{6,7},{7,6},{8,9},{9,8},{10,11... | collective-permute-start | bytes 393224 | tf_op jit(solution)/shard_map/ppermute | solution.py:414
  71.6 9.6 %collective-permute-start.20 = (bf16[256,512]{1,0:T(8,128)(2,1)S(1)}, bf16[256,512]{1,0:T(8,128)(2,1)S(1)}, u32[]{:S(2)}, u32[]{:S(2)}) collective-permute-start(bf16[256,512]{1,0:T(8,128)(2,1)S(1)} %bitcast.3), channel_id=1, source_target_pairs={{0,2},{1,3},{2,0},{3,1},{4,6},{5,7},{6,4},{7,5},{8,10},{9,11},{10,... | collective-permute-start | bytes 786440 | tf_op jit(solution)/shard_map/ppermute | solution.py:417

commit v4 on v3

--- a/solution.py
+++ b/solution.py
@@ -400,23 +400,52 @@
         [(2 * y + k, 2 * ((y + d) % ys) + k) for y in range(ys) for k in range(2)] for d in range(1, ys)
     ]
 
-    finished = []
-    for piece in range(NUW):
-        came = lax.ppermute(made[2 * piece + 1], "row", swap_pair)
-        near, far = pair_section(made[2 * piece], came)
-        parts = [lax.ppermute(far, "row", moves) for moves in inward[1]]
-        parts += [lax.ppermute(near, "row", moves) for moves in inward[0]]
-        host = line_section([near, *parts])
-        held = [host] + [lax.ppermute(host, "row", moves) for moves in outward]
-        own, away = owned_section(plan, held)
-        fix = lax.ppermute(away, "row", swap_pair)
-        own_core = lax.ppermute(own, "col", swap_core)
+    state = [{"came": [lax.ppermute(made[2 * p + 1], "row", swap_pair)]} for p in range(NUW)]
+    moves_in = [*inward[1], *inward[0]]
+
+    def pair(p, now):
+        near, far = pair_section(made[2 * p], *now["came"])
+        sources = [far] * half + [near] * (half - 1)
+        order = (2, 0, 1) if len(moves_in) == len((2, 0, 1)) else range(len(moves_in))
+        now["near"] = near
+        now["came"] = [lax.ppermute(sources[k], "row", moves_in[k]) for k in order]
+        return near
+
+    def line(p, now):
+        now["host"] = line_section([now["near"], *now["came"]])
+        now["came"] = [lax.ppermute(now["host"], "row", m) for m in outward]
+        return now["host"]
+
+    def owned(p, now):
+        now["own"], away = owned_section(plan, [now["host"], *now["came"]])
+        now["came"] = [lax.ppermute(away, "row", swap_pair)]
+        now["own_core"] = lax.ppermute(now["own"], "col", swap_core)
+        return away
+
+    def term(p, now):
+        (fix,) = now["came"]
         fix_core = lax.ppermute(fix, "col", swap_core)
-        sent, kept = term_section(keep, got, own, own_core, fix, fix_core)
-        for d in range(1, ys):
-            kept = kept + lax.ppermute(sent[d - 1], "col", around[d - 1]).astype(jnp.float32)
-        finished.append(kept.astype(jnp.bfloat16))
-    return jnp.concatenate(finished, axis=1)
+        sent, now["kept"] = term_section(keep, got, now["own"], now["own_core"], fix, fix_core)
+        now["came"] = [lax.ppermute(sent[d - 1], "col", around[d - 1]) for d in range(1, ys)]
+        return now["kept"]
+
+    def finish(p, now):
+        for part in now["came"]:
+            now["kept"] = now["kept"] + part.astype(jnp.float32)
+        now["kept"] = now["kept"].astype(jnp.bfloat16)
+        return now["kept"]
+
+    stages = [pair, line, owned, term, finish]
+    order = ((0, 0), (0, 1), (1, 0), (2, 0), (3, 0), (4, 0), (1, 1), (2, 1), (3, 1), (4, 1))
+    after = {(1, 0): [(0, 1)], (2, 0): [(0, 1)]}
+    token = {}
+    for index, p in order:
+        now = state[p]
+        if (index, p) in after:
+            gated = lax.optimization_barrier((*now["came"], *[token[t] for t in after[index, p]]))
+            now["came"] = list(gated[: len(now["came"])])
+        token[index, p] = stages[index](p, now)
+    return jnp.concatenate([now["kept"] for now in state], axis=1)
 
 
 def solution(mesh):

time: 82.4 us -> 79.7 us (0.967)
  waiting for transfers between devices: 38.4 us -> 31.6 us
  starting transfers between devices: 27.2 us -> 30.6 us
    ppermute x20, waiting for transfers between devices: 38.4 us -> 31.6 us  [the longest x2 11.5 us: per_device(): lax.ppermute(made[2 * p + 1], 'row', swap_pair)]
    ppermute x20, starting transfers between devices: 27.1 us -> 30.5 us  [the longest x6 17.1 us: pair(): now['came'] = [lax.ppermute(sources[k], 'row', moves_in[k]) for k in order]]
  transfers between devices with their start and end apart: 21 -> 21, of which waited for: 10 -> 10; matrix products, arithmetic and copies ran while one was open for 0% -> 0% of each run, Pallas kernels for 7% -> 8%
where the time goes in v4:
time: 79.7 us; the launch traced here: 78.7 us
  waiting for transfers between devices  31.6 us (40%)
  starting transfers between devices  30.6 us (38%)
  Pallas kernels  13.6 us (17%)
  local copies, waits for them, and re-layouts  1.62 us (2%)
  other arithmetic  1.01 us (1%)
    ppermute x6, starting transfers between devices, pair(): now['came'] = [lax.ppermute(sources[k], 'row', moves_in[k]) for k in order]  17.1 us
    ppermute x2, waiting for transfers between devices, per_device(): lax.ppermute(made[2 * p + 1], 'row', swap_pair)  11.5 us
    ppermute x2, waiting for transfers between devices, term(): lax.ppermute(sent[d - 1], 'col', around[d - 1])  7.82 us
    pallas_call x1, Pallas kernels, first_section(): pl.pallas_call(functools.partial(first_kernel, rows, table, group), in_sp...  7.63 us
    ppermute x2, waiting for transfers between devices, owned(): now['came'] = [lax.ppermute(away, 'row', swap_pair)]  4.87 us
    ppermute x4, waiting for transfers between devices, line(): now['came'] = [lax.ppermute(now['host'], 'row', m) for m in outward]  4.12 us
    ppermute x4, starting transfers between devices, line(): now['came'] = [lax.ppermute(now['host'], 'row', m) for m in outward]  3.94 us
    ppermute x2, starting transfers between devices, term(): lax.ppermute(sent[d - 1], 'col', around[d - 1])  3.18 us
  transfers between devices with their start and end apart: 21, of which 10 were waited for; matrix products, arithmetic and copies ran while one was open for 0% of the time, Pallas kernels for 8%

profile of v4, /device:TPU:0, one launch (start us, length us, event | category | flops | bytes accessed | tf_op | source)
XLA Modules:
  0.0 78.7 jit_solution(8681117044265823294)
XLA Ops:
  0.0 7.6 %first_section.1 = (bf16[4,128,512]{2,1,0:T(8,128)(2,1)}, bf16[4,128,512]{2,1,0:T(8,128)(2,1)}, s32[4]{0:T(128)}, bf16[8,128,1024]{2,1,0:T(8,128)(2,1)}) custom-call(s32[160]{0:T(256)} %aux_in.1, s32[160]{0:T(256)} %ao_in.1, s32[1,8]{1,0:T(1,128)} %owner_in.1, bf16[160,256,128]{2,1,0:T(8,128)(2,1)} %tiles_in.1, bf16[1024,512]{1,0:T(8,128)(2,1)} %coeff.1), custom_call_target="tpu_custom_call" | custom-call | flops 1073741824 | bytes 11534336 | tf_op jit(solution)/shard_map/first_section/pallas_call | solution.py:163
  7.6 0.0 copy-start.2
  7.7 3.0 %collective-permute-start.1 = (bf16[4,128,512]{2,1,0:T(8,128)(2,1)}, bf16[4,128,512]{2,1,0:T(8,128)(2,1)S(1)}, u32[]{:S(2)}, u32[]{:S(2)}) collective-permute-start(bf16[4,128,512]{2,1,0:T(8,128)(2,1)} %get-tuple-element.34), channel_id=1, source_target_pairs={{0,4},{4,0},{8,12},{12,8},{16,20},{20,16},{24,28},{28,24},{1,5},{5... | collective-permute-start | bytes 1572872 | tf_op jit(solution)/shard_map/ppermute | solution.py:403
  10.7 1.6 %copy-done.6 = bf16[8,128,1024]{2,1,0:T(8,128)(2,1)S(1)} copy-done((bf16[8,128,1024]{2,1,0:T(8,128)(2,1)S(1)}, bf16[8,128,1024]{2,1,0:T(8,128)(2,1)}, u32[]{:S(2)}) %copy-start.6) | copy-done | bytes 2097176
  12.3 1.2 %later_section.1 = (bf16[4,128,512]{2,1,0:T(8,128)(2,1)S(1)}, bf16[4,128,512]{2,1,0:T(8,128)(2,1)S(1)}) custom-call(bf16[8,128,1024]{2,1,0:T(8,128)(2,1)S(1)} %copy-done.6, bf16[1024,512]{1,0:T(8,128)(2,1)S(1)} %copy-done.1), custom_call_target="tpu_custom_call" | custom-call | flops 1073741824 | bytes 4194304 | tf_op jit(solution)/shard_map/later_section/pallas_call | solution.py:210
  13.5 0.0 copy-start
  13.5 0.0 copy-start.4
  13.5 0.0 copy-start.5
  13.6 0.1 collective-permute-start.5
  13.7 9.9 %collective-permute-done.1.came = bf16[4,128,512]{2,1,0:T(8,128)(2,1)S(1)} collective-permute-done((bf16[4,128,512]{2,1,0:T(8,128)(2,1)}, bf16[4,128,512]{2,1,0:T(8,128)(2,1)S(1)}, u32[]{:S(2)}, u32[]{:S(2)}) %collective-permute-start.1) | collective-permute-done | bytes 524320 | tf_op jit(solution)/shard_map/ppermute | solution.py:403
  23.6 0.0 copy-done.2
  23.6 0.1 pair_section.2
  23.8 4.1 %collective-permute-start.2 = (bf16[2,128,512]{2,1,0:T(8,128)(2,1)S(1)}, bf16[2,128,512]{2,1,0:T(8,128)(2,1)S(1)}, u32[]{:S(2)}, u32[]{:S(2)}) collective-permute-start(bf16[2,128,512]{2,1,0:T(8,128)(2,1)S(1)} %get-tuple-element.35.refs_0_), channel_id=1, source_target_pairs={{0,8},{4,12},{24,16},{28,20},{1,9},{5,13},{25,17},{29,21},{2,10},{... | collective-permute-start | bytes 786440 | tf_op jit(solution)/shard_map/ppermute | solution.py:411
  27.8 0.7 collective-permute-start.3
  28.5 4.0 %collective-permute-start.4 = (bf16[2,128,512]{2,1,0:T(8,128)(2,1)S(1)}, bf16[2,128,512]{2,1,0:T(8,128)(2,1)S(1)}, u32[]{:S(2)}, u32[]{:S(2)}) collective-permute-start(bf16[2,128,512]{2,1,0:T(8,128)(2,1)S(1)} %get-tuple-element.36), channel_id=1, source_target_pairs={{0,16},{4,20},{24,8},{28,12},{1,17},{5,21},{25,9},{29,13},{2,18},{... | collective-permute-start | bytes 786440 | tf_op jit(solution)/shard_map/ppermute | solution.py:411
  32.5 1.5 %collective-permute-done.5.came = bf16[4,128,512]{2,1,0:T(8,128)(2,1)S(1)} collective-permute-done((bf16[4,128,512]{2,1,0:T(8,128)(2,1)S(1)}, bf16[4,128,512]{2,1,0:T(8,128)(2,1)S(1)}, u32[]{:S(2)}, u32[]{:S(2)}) %collective-permute-start.5) | collective-permute-done | bytes 524320 | tf_op jit(solution)/shard_map/ppermute | solution.py:403
  34.0 0.1 pair_section.3
  34.2 3.7 %collective-permute-start.12 = (bf16[2,128,512]{2,1,0:T(8,128)(2,1)S(1)}, bf16[2,128,512]{2,1,0:T(8,128)(2,1)S(1)}, u32[]{:S(2)}, u32[]{:S(2)}) collective-permute-start(bf16[2,128,512]{2,1,0:T(8,128)(2,1)S(1)} %get-tuple-element.40.refs_0_), channel_id=1, source_target_pairs={{0,8},{4,12},{24,16},{28,20},{1,9},{5,13},{25,17},{29,21},{2,10},{... | collective-permute-start | bytes 786440 | tf_op jit(solution)/shard_map/ppermute | solution.py:411
  37.9 0.7 collective-permute-start.13
  38.6 0.0 collective-permute-done.2.refs_1_
  38.6 4.0 %collective-permute-start.14 = (bf16[2,128,512]{2,1,0:T(8,128)(2,1)S(1)}, bf16[2,128,512]{2,1,0:T(8,128)(2,1)S(1)}, u32[]{:S(2)}, u32[]{:S(2)}) collective-permute-start(bf16[2,128,512]{2,1,0:T(8,128)(2,1)S(1)} %get-tuple-element.50), channel_id=1, source_target_pairs={{0,16},{4,20},{24,8},{28,12},{1,17},{5,21},{25,9},{29,13},{2,18},{... | collective-permute-start | bytes 786440 | tf_op jit(solution)/shard_map/ppermute | solution.py:411
  42.6 0.0 collective-permute-done.3.refs_2_
  42.6 0.0 collective-permute-done.4.refs_3_
  42.6 0.1 line_section.2.refs_0_
  42.8 1.3 %collective-permute-start.6 = (bf16[2,128,512]{2,1,0:T(8,128)(2,1)S(1)}, bf16[2,128,512]{2,1,0:T(8,128)(2,1)S(1)}, u32[]{:S(2)}, u32[]{:S(2)}) collective-permute-start(bf16[2,128,512]{2,1,0:T(8,128)(2,1)S(1)} %line_section.2.refs_0_), channel_id=1, source_target_pairs={{8,0},{12,4},{16,24},{20,28},{9,1},{13,5},{17,25},{21,29},{10,2},{... | collective-permute-start | bytes 786440 | tf_op jit(solution)/shard_map/ppermute | solution.py:416
  44.1 0.7 collective-permute-start.7
  44.7 0.0 copy-done
  44.8 0.0 copy-done.3
  44.8 1.8 %metric_section.1 = (bf16[2,256,384]{2,1,0:T(8,128)(2,1)S(1)}, bf16[2,256,384]{2,1,0:T(8,128)(2,1)S(1)}) custom-call(s32[4]{0:T(128)S(1)} %copy-done.3, s32[64]{0:T(128)S(1)} %copy-done.4, s32[64]{0:T(128)S(1)} %copy-done.5, bf16[64,128,128]{2,1,0:T(8,128)(2,1)S(1)} %copy-done), custom_call_target="tpu_custom_call" | custom-call | bytes 3697152 | tf_op jit(solution)/shard_map/metric_section/pallas_call | solution.py:247
  46.6 0.0 collective-permute-done.12.refs_1_
  46.6 0.1 collective-permute-start
  46.7 0.0 collective-permute-done.13.refs_2_
  46.7 1.9 %collective-permute-done.14.refs_3_ = bf16[2,128,512]{2,1,0:T(8,128)(2,1)S(1)} collective-permute-done((bf16[2,128,512]{2,1,0:T(8,128)(2,1)S(1)}, bf16[2,128,512]{2,1,0:T(8,128)(2,1)S(1)}, u32[]{:S(2)}, u32[]{:S(2)}) %collective-permute-start.14) | collective-permute-done | bytes 262176 | tf_op jit(solution)/shard_map/ppermute | solution.py:411
  48.6 0.1 line_section.3.refs_0_
  48.8 1.3 %collective-permute-start.15 = (bf16[2,128,512]{2,1,0:T(8,128)(2,1)S(1)}, bf16[2,128,512]{2,1,0:T(8,128)(2,1)S(1)}, u32[]{:S(2)}, u32[]{:S(2)}) collective-permute-start(bf16[2,128,512]{2,1,0:T(8,128)(2,1)S(1)} %line_section.3.refs_0_), channel_id=1, source_target_pairs={{8,0},{12,4},{16,24},{20,28},{9,1},{13,5},{17,25},{21,29},{10,2},{... | collective-permute-start | bytes 786440 | tf_op jit(solution)/shard_map/ppermute | solution.py:416
  50.1 0.7 collective-permute-start.16
  50.7 0.5 collective-permute-done.6.refs_1_
  51.3 0.0 collective-permute-done.7.refs_2_
  51.3 0.6 owned_section.2
  51.9 1.6 %collective-permute-start.9 = (bf16[1,128,512]{2,1,0:T(8,128)(2,1)S(1)}, bf16[1,128,512]{2,1,0:T(8,128)(2,1)S(1)}, u32[]{:S(2)}, u32[]{:S(2)}) collective-permute-start(bf16[1,128,512]{2,1,0:T(8,128)(2,1)S(1)} %get-tuple-element.47), channel_id=1, source_target_pairs={{0,4},{4,0},{8,12},{12,8},{16,20},{20,16},{24,28},{28,24},{1,5},{5... | collective-permute-start | bytes 393224 | tf_op jit(solution)/shard_map/ppermute | solution.py:421
  53.5 0.0 collective-permute-start.8
  53.5 3.5 %collective-permute-done.9.fix = bf16[1,128,512]{2,1,0:T(8,128)(2,1)S(1)} collective-permute-done((bf16[1,128,512]{2,1,0:T(8,128)(2,1)S(1)}, bf16[1,128,512]{2,1,0:T(8,128)(2,1)S(1)}, u32[]{:S(2)}, u32[]{:S(2)}) %collective-permute-start.9) | collective-permute-done | bytes 131104 | tf_op jit(solution)/shard_map/ppermute | solution.py:421
  56.9 0.0 collective-permute-start.10
  56.9 3.6 %collective-permute-done.15.refs_1_ = bf16[2,128,512]{2,1,0:T(8,128)(2,1)S(1)} collective-permute-done((bf16[2,128,512]{2,1,0:T(8,128)(2,1)S(1)}, bf16[2,128,512]{2,1,0:T(8,128)(2,1)S(1)}, u32[]{:S(2)}, u32[]{:S(2)}) %collective-permute-start.15) | collective-permute-done | bytes 262176 | tf_op jit(solution)/shard_map/ppermute | solution.py:416
  60.5 0.0 collective-permute-done.16.refs_2_
  60.5 0.6 owned_section.3
  61.2 1.6 %collective-permute-start.18 = (bf16[1,128,512]{2,1,0:T(8,128)(2,1)S(1)}, bf16[1,128,512]{2,1,0:T(8,128)(2,1)S(1)}, u32[]{:S(2)}, u32[]{:S(2)}) collective-permute-start(bf16[1,128,512]{2,1,0:T(8,128)(2,1)S(1)} %get-tuple-element.52), channel_id=1, source_target_pairs={{0,4},{4,0},{8,12},{12,8},{16,20},{20,16},{24,28},{28,24},{1,5},{5... | collective-permute-start | bytes 393224 | tf_op jit(solution)/shard_map/ppermute | solution.py:421
  62.7 0.0 collective-permute-start.17
  62.7 0.0 collective-permute-done.got
  62.7 0.0 collective-permute-done.10.fix_core
  62.7 0.0 collective-permute-done.8.own_core
  62.7 0.6 term_section.2
  63.3 1.6 %collective-permute-start.11 = (bf16[256,512]{1,0:T(8,128)(2,1)S(1)}, bf16[256,512]{1,0:T(8,128)(2,1)S(1)}, u32[]{:S(2)}, u32[]{:S(2)}) collective-permute-start(bf16[256,512]{1,0:T(8,128)(2,1)S(1)} %bitcast.2), channel_id=1, source_target_pairs={{0,2},{1,3},{2,0},{3,1},{4,6},{5,7},{6,4},{7,5},{8,10},{9,11},{10,... | collective-permute-start | bytes 786440 | tf_op jit(solution)/shard_map/ppermute | solution.py:429
  64.9 1.4 %collective-permute-done.18.fix = bf16[1,128,512]{2,1,0:T(8,128)(2,1)S(1)} collective-permute-done((bf16[1,128,512]{2,1,0:T(8,128)(2,1)S(1)}, bf16[1,128,512]{2,1,0:T(8,128)(2,1)S(1)}, u32[]{:S(2)}, u32[]{:S(2)}) %collective-permute-start.18) | collective-permute-done | bytes 131104 | tf_op jit(solution)/shard_map/ppermute | solution.py:421
  66.3 0.0 collective-permute-start.19
  66.3 1.3 %collective-permute-done.19.fix_core = bf16[1,128,512]{2,1,0:T(8,128)(2,1)S(1)} collective-permute-done((bf16[1,128,512]{2,1,0:T(8,128)(2,1)S(1)}, bf16[1,128,512]{2,1,0:T(8,128)(2,1)S(1)}, u32[]{:S(2)}, u32[]{:S(2)}) %collective-permute-start.19) | collective-permute-done | bytes 131104 | tf_op jit(solution)/shard_map/ppermute | solution.py:427
  67.6 0.0 collective-permute-done.17.own_core
  67.7 0.6 term_section.3
  68.2 1.6 %collective-permute-start.20 = (bf16[256,512]{1,0:T(8,128)(2,1)S(1)}, bf16[256,512]{1,0:T(8,128)(2,1)S(1)}, u32[]{:S(2)}, u32[]{:S(2)}) collective-permute-start(bf16[256,512]{1,0:T(8,128)(2,1)S(1)} %bitcast.3), channel_id=1, source_target_pairs={{0,2},{1,3},{2,0},{3,1},{4,6},{5,7},{6,4},{7,5},{8,10},{9,11},{10,... | collective-permute-start | bytes 786440 | tf_op jit(solution)/shard_map/ppermute | solution.py:429
  69.8 2.7 %collective-permute-done.11 = bf16[256,512]{1,0:T(8,128)(2,1)S(1)} collective-permute-done((bf16[256,512]{1,0:T(8,128)(2,1)S(1)}, bf16[256,512]{1,0:T(8,128)(2,1)S(1)}, u32[]{:S(2)}, u32[]{:S(2)}) %collective-permute-start.11) | collective-permute-done | bytes 262176 | tf_op jit(solution)/shard_map/ppermute | solution.py:429
  72.5 0.1 add_convert_fusion.1
  72.6 5.2 %collective-permute-done.20 = bf16[256,512]{1,0:T(8,128)(2,1)S(1)} collective-permute-done((bf16[256,512]{1,0:T(8,128)(2,1)S(1)}, bf16[256,512]{1,0:T(8,128)(2,1)S(1)}, u32[]{:S(2)}, u32[]{:S(2)}) %collective-permute-start.20) | collective-permute-done | bytes 262176 | tf_op jit(solution)/shard_map/ppermute | solution.py:429
  77.7 0.1 add_convert_fusion
  77.8 0.9 %pad_maximum_fusion = bf16[256,1024]{1,0:T(8,128)(2,1)} fusion(bf16[256,512]{1,0:T(8,128)(2,1)S(1)} %add_convert_fusion, bf16[256,512]{1,0:T(8,128)(2,1)S(1)} %add_convert_fusion.1), kind=kLoop, calls=%fused_computation | loop fusion | flops 1048576 | bytes 1048576 | tf_op jit(solution)/shard_map/concatenate | solution.py:448
  (6 shorter events, 0.0 us)
Async XLA Ops:
  0.0 10.7 %copy-start.1 = (bf16[1024,512]{1,0:T(8,128)(2,1)S(1)}, bf16[1024,512]{1,0:T(8,128)(2,1)}, u32[]{:S(2)}) copy-start(bf16[1024,512]{1,0:T(8,128)(2,1)} %coeff.1) | copy-start | bytes 3145732
  7.6 16.0 %copy-start.2 = (bf16[4,128,512]{2,1,0:T(8,128)(2,1)S(1)}, bf16[4,128,512]{2,1,0:T(8,128)(2,1)}, u32[]{:S(2)}) copy-start(bf16[4,128,512]{2,1,0:T(8,128)(2,1)} %get-tuple-element.33.mine) | copy-start | bytes 1572868
  7.7 16.0 %collective-permute-start.1 = (bf16[4,128,512]{2,1,0:T(8,128)(2,1)}, bf16[4,128,512]{2,1,0:T(8,128)(2,1)S(1)}, u32[]{:S(2)}, u32[]{:S(2)}) collective-permute-start(bf16[4,128,512]{2,1,0:T(8,128)(2,1)} %get-tuple-element.34), channel_id=1, source_target_pairs={{0,4},{4,0},{8,12},{12,8},{16,20},{20,16},{24,28},{28,24},{1,5},{5... | collective-permute-start | bytes 1572872 | tf_op jit(solution)/shard_map/ppermute | solution.py:403
  10.7 1.6 %copy-start.6 = (bf16[8,128,1024]{2,1,0:T(8,128)(2,1)S(1)}, bf16[8,128,1024]{2,1,0:T(8,128)(2,1)}, u32[]{:S(2)}) copy-start(bf16[8,128,1024]{2,1,0:T(8,128)(2,1)} %get-tuple-element.37.left) | copy-start | bytes 6291460
  13.5 31.2 %copy-start = (bf16[64,128,128]{2,1,0:T(8,128)(2,1)S(1)}, bf16[64,128,128]{2,1,0:T(8,128)(2,1)}, u32[]{:S(2)}) copy-start(bf16[64,128,128]{2,1,0:T(8,128)(2,1)} %metric.1) | copy-start | bytes 6291460
  13.5 31.2 %copy-start.3 = (s32[4]{0:T(128)S(1)}, s32[4]{0:T(128)}, u32[]{:S(2)}) copy-start(s32[4]{0:T(128)} %get-tuple-element.30.plan) | copy-start | bytes 52
  13.5 31.2 %copy-start.4 = (s32[64]{0:T(128)S(1)}, s32[64]{0:T(128)}, u32[]{:S(2)}) copy-start(s32[64]{0:T(128)} %slots.1) | copy-start | bytes 772
  13.5 31.2 %copy-start.5 = (s32[64]{0:T(128)S(1)}, s32[64]{0:T(128)}, u32[]{:S(2)}) copy-start(s32[64]{0:T(128)} %outs_of.1) | copy-start | bytes 772
  13.6 20.5 %collective-permute-start.5 = (bf16[4,128,512]{2,1,0:T(8,128)(2,1)S(1)}, bf16[4,128,512]{2,1,0:T(8,128)(2,1)S(1)}, u32[]{:S(2)}, u32[]{:S(2)}) collective-permute-start(bf16[4,128,512]{2,1,0:T(8,128)(2,1)S(1)} %get-tuple-element.39), channel_id=1, source_target_pairs={{0,4},{4,0},{8,12},{12,8},{16,20},{20,16},{24,28},{28,24},{1,5},{5... | collective-permute-start | bytes 1572872 | tf_op jit(solution)/shard_map/ppermute | solution.py:403
  23.8 14.8 %collective-permute-start.2 = (bf16[2,128,512]{2,1,0:T(8,128)(2,1)S(1)}, bf16[2,128,512]{2,1,0:T(8,128)(2,1)S(1)}, u32[]{:S(2)}, u32[]{:S(2)}) collective-permute-start(bf16[2,128,512]{2,1,0:T(8,128)(2,1)S(1)} %get-tuple-element.35.refs_0_), channel_id=1, source_target_pairs={{0,8},{4,12},{24,16},{28,20},{1,9},{5,13},{25,17},{29,21},{2,10},{... | collective-permute-start | bytes 786440 | tf_op jit(solution)/shard_map/ppermute | solution.py:411
  27.8 14.8 %collective-permute-start.3 = (bf16[2,128,512]{2,1,0:T(8,128)(2,1)S(1)}, bf16[2,128,512]{2,1,0:T(8,128)(2,1)S(1)}, u32[]{:S(2)}, u32[]{:S(2)}) collective-permute-start(bf16[2,128,512]{2,1,0:T(8,128)(2,1)S(1)} %get-tuple-element.36), channel_id=1, source_target_pairs={{8,16},{12,20},{16,8},{20,12},{9,17},{13,21},{17,9},{21,13},{10,18... | collective-permute-start | bytes 786440 | tf_op jit(solution)/shard_map/ppermute | solution.py:411
  28.5 14.1 %collective-permute-start.4 = (bf16[2,128,512]{2,1,0:T(8,128)(2,1)S(1)}, bf16[2,128,512]{2,1,0:T(8,128)(2,1)S(1)}, u32[]{:S(2)}, u32[]{:S(2)}) collective-permute-start(bf16[2,128,512]{2,1,0:T(8,128)(2,1)S(1)} %get-tuple-element.36), channel_id=1, source_target_pairs={{0,16},{4,20},{24,8},{28,12},{1,17},{5,21},{25,9},{29,13},{2,18},{... | collective-permute-start | bytes 786440 | tf_op jit(solution)/shard_map/ppermute | solution.py:411
  34.2 12.4 %collective-permute-start.12 = (bf16[2,128,512]{2,1,0:T(8,128)(2,1)S(1)}, bf16[2,128,512]{2,1,0:T(8,128)(2,1)S(1)}, u32[]{:S(2)}, u32[]{:S(2)}) collective-permute-start(bf16[2,128,512]{2,1,0:T(8,128)(2,1)S(1)} %get-tuple-element.40.refs_0_), channel_id=1, source_target_pairs={{0,8},{4,12},{24,16},{28,20},{1,9},{5,13},{25,17},{29,21},{2,10},{... | collective-permute-start | bytes 786440 | tf_op jit(solution)/shard_map/ppermute | solution.py:411
  37.9 8.8 %collective-permute-start.13 = (bf16[2,128,512]{2,1,0:T(8,128)(2,1)S(1)}, bf16[2,128,512]{2,1,0:T(8,128)(2,1)S(1)}, u32[]{:S(2)}, u32[]{:S(2)}) collective-permute-start(bf16[2,128,512]{2,1,0:T(8,128)(2,1)S(1)} %get-tuple-element.50), channel_id=1, source_target_pairs={{8,16},{12,20},{16,8},{20,12},{9,17},{13,21},{17,9},{21,13},{10,18... | collective-permute-start | bytes 786440 | tf_op jit(solution)/shard_map/ppermute | solution.py:411
  38.6 10.0 %collective-permute-start.14 = (bf16[2,128,512]{2,1,0:T(8,128)(2,1)S(1)}, bf16[2,128,512]{2,1,0:T(8,128)(2,1)S(1)}, u32[]{:S(2)}, u32[]{:S(2)}) collective-permute-start(bf16[2,128,512]{2,1,0:T(8,128)(2,1)S(1)} %get-tuple-element.50), channel_id=1, source_target_pairs={{0,16},{4,20},{24,8},{28,12},{1,17},{5,21},{25,9},{29,13},{2,18},{... | collective-permute-start | bytes 786440 | tf_op jit(solution)/shard_map/ppermute | solution.py:411
  42.8 8.5 %collective-permute-start.6 = (bf16[2,128,512]{2,1,0:T(8,128)(2,1)S(1)}, bf16[2,128,512]{2,1,0:T(8,128)(2,1)S(1)}, u32[]{:S(2)}, u32[]{:S(2)}) collective-permute-start(bf16[2,128,512]{2,1,0:T(8,128)(2,1)S(1)} %line_section.2.refs_0_), channel_id=1, source_target_pairs={{8,0},{12,4},{16,24},{20,28},{9,1},{13,5},{17,25},{21,29},{10,2},{... | collective-permute-start | bytes 786440 | tf_op jit(solution)/shard_map/ppermute | solution.py:416
  44.1 7.2 %collective-permute-start.7 = (bf16[2,128,512]{2,1,0:T(8,128)(2,1)S(1)}, bf16[2,128,512]{2,1,0:T(8,128)(2,1)S(1)}, u32[]{:S(2)}, u32[]{:S(2)}) collective-permute-start(bf16[2,128,512]{2,1,0:T(8,128)(2,1)S(1)} %line_section.2.refs_0_), channel_id=1, source_target_pairs={{8,16},{12,20},{16,8},{20,12},{9,17},{13,21},{17,9},{21,13},{10,18... | collective-permute-start | bytes 786440 | tf_op jit(solution)/shard_map/ppermute | solution.py:416
  46.6 16.1 %collective-permute-start = (bf16[2,256,384]{2,1,0:T(8,128)(2,1)S(1)}, bf16[2,256,384]{2,1,0:T(8,128)(2,1)S(1)}, u32[]{:S(2)}, u32[]{:S(2)}) collective-permute-start(bf16[2,256,384]{2,1,0:T(8,128)(2,1)S(1)} %get-tuple-element.32), channel_id=1, source_target_pairs={{0,1},{1,0},{2,3},{3,2},{4,5},{5,4},{6,7},{7,6},{8,9},{9,8},{10,11... | collective-permute-start | bytes 1179656 | tf_op jit(solution)/shard_map/ppermute | solution.py:389
  48.8 11.8 %collective-permute-start.15 = (bf16[2,128,512]{2,1,0:T(8,128)(2,1)S(1)}, bf16[2,128,512]{2,1,0:T(8,128)(2,1)S(1)}, u32[]{:S(2)}, u32[]{:S(2)}) collective-permute-start(bf16[2,128,512]{2,1,0:T(8,128)(2,1)S(1)} %line_section.3.refs_0_), channel_id=1, source_target_pairs={{8,0},{12,4},{16,24},{20,28},{9,1},{13,5},{17,25},{21,29},{10,2},{... | collective-permute-start | bytes 786440 | tf_op jit(solution)/shard_map/ppermute | solution.py:416
  50.1 10.5 %collective-permute-start.16 = (bf16[2,128,512]{2,1,0:T(8,128)(2,1)S(1)}, bf16[2,128,512]{2,1,0:T(8,128)(2,1)S(1)}, u32[]{:S(2)}, u32[]{:S(2)}) collective-permute-start(bf16[2,128,512]{2,1,0:T(8,128)(2,1)S(1)} %line_section.3.refs_0_), channel_id=1, source_target_pairs={{8,16},{12,20},{16,8},{20,12},{9,17},{13,21},{17,9},{21,13},{10,18... | collective-permute-start | bytes 786440 | tf_op jit(solution)/shard_map/ppermute | solution.py:416
  51.9 5.0 %collective-permute-start.9 = (bf16[1,128,512]{2,1,0:T(8,128)(2,1)S(1)}, bf16[1,128,512]{2,1,0:T(8,128)(2,1)S(1)}, u32[]{:S(2)}, u32[]{:S(2)}) collective-permute-start(bf16[1,128,512]{2,1,0:T(8,128)(2,1)S(1)} %get-tuple-element.47), channel_id=1, source_target_pairs={{0,4},{4,0},{8,12},{12,8},{16,20},{20,16},{24,28},{28,24},{1,5},{5... | collective-permute-start | bytes 393224 | tf_op jit(solution)/shard_map/ppermute | solution.py:421
  53.5 9.3 %collective-permute-start.8 = (bf16[2,128,512]{2,1,0:T(8,128)(2,1)S(1)}, bf16[2,128,512]{2,1,0:T(8,128)(2,1)S(1)}, u32[]{:S(2)}, u32[]{:S(2)}) collective-permute-start(bf16[2,128,512]{2,1,0:T(8,128)(2,1)S(1)} %get-tuple-element.46.own), channel_id=1, source_target_pairs={{0,1},{1,0},{2,3},{3,2},{4,5},{5,4},{6,7},{7,6},{8,9},{9,8},{10,11... | collective-permute-start | bytes 786440 | tf_op jit(solution)/shard_map/ppermute | solution.py:422
  56.9 5.8 %collective-permute-start.10 = (bf16[1,128,512]{2,1,0:T(8,128)(2,1)S(1)}, bf16[1,128,512]{2,1,0:T(8,128)(2,1)S(1)}, u32[]{:S(2)}, u32[]{:S(2)}) collective-permute-start(bf16[1,128,512]{2,1,0:T(8,128)(2,1)S(1)} %collective-permute-done.9.fix), channel_id=1, source_target_pairs={{0,1},{1,0},{2,3},{3,2},{4,5},{5,4},{6,7},{7,6},{8,9},{9,8},{10,11... | collective-permute-start | bytes 393224 | tf_op jit(solution)/shard_map/ppermute | solution.py:427
  61.2 5.1 %collective-permute-start.18 = (bf16[1,128,512]{2,1,0:T(8,128)(2,1)S(1)}, bf16[1,128,512]{2,1,0:T(8,128)(2,1)S(1)}, u32[]{:S(2)}, u32[]{:S(2)}) collective-permute-start(bf16[1,128,512]{2,1,0:T(8,128)(2,1)S(1)} %get-tuple-element.52), channel_id=1, source_target_pairs={{0,4},{4,0},{8,12},{12,8},{16,20},{20,16},{24,28},{28,24},{1,5},{5... | collective-permute-start | bytes 393224 | tf_op jit(solution)/shard_map/ppermute | solution.py:421
  62.7 4.9 %collective-permute-start.17 = (bf16[2,128,512]{2,1,0:T(8,128)(2,1)S(1)}, bf16[2,128,512]{2,1,0:T(8,128)(2,1)S(1)}, u32[]{:S(2)}, u32[]{:S(2)}) collective-permute-start(bf16[2,128,512]{2,1,0:T(8,128)(2,1)S(1)} %get-tuple-element.51.own), channel_id=1, source_target_pairs={{0,1},{1,0},{2,3},{3,2},{4,5},{5,4},{6,7},{7,6},{8,9},{9,8},{10,11... | collective-permute-start | bytes 786440 | tf_op jit(solution)/shard_map/ppermute | solution.py:422
  63.3 9.2 %collective-permute-start.11 = (bf16[256,512]{1,0:T(8,128)(2,1)S(1)}, bf16[256,512]{1,0:T(8,128)(2,1)S(1)}, u32[]{:S(2)}, u32[]{:S(2)}) collective-permute-start(bf16[256,512]{1,0:T(8,128)(2,1)S(1)} %bitcast.2), channel_id=1, source_target_pairs={{0,2},{1,3},{2,0},{3,1},{4,6},{5,7},{6,4},{7,5},{8,10},{9,11},{10,... | collective-permute-start | bytes 786440 | tf_op jit(solution)/shard_map/ppermute | solution.py:429
  66.3 1.3 %collective-permute-start.19 = (bf16[1,128,512]{2,1,0:T(8,128)(2,1)S(1)}, bf16[1,128,512]{2,1,0:T(8,128)(2,1)S(1)}, u32[]{:S(2)}, u32[]{:S(2)}) collective-permute-start(bf16[1,128,512]{2,1,0:T(8,128)(2,1)S(1)} %collective-permute-done.18.fix), channel_id=1, source_target_pairs={{0,1},{1,0},{2,3},{3,2},{4,5},{5,4},{6,7},{7,6},{8,9},{9,8},{10,11... | collective-permute-start | bytes 393224 | tf_op jit(solution)/shard_map/ppermute | solution.py:427
  68.2 9.5 %collective-permute-start.20 = (bf16[256,512]{1,0:T(8,128)(2,1)S(1)}, bf16[256,512]{1,0:T(8,128)(2,1)S(1)}, u32[]{:S(2)}, u32[]{:S(2)}) collective-permute-start(bf16[256,512]{1,0:T(8,128)(2,1)S(1)} %bitcast.3), channel_id=1, source_target_pairs={{0,2},{1,3},{2,0},{3,1},{4,6},{5,7},{6,4},{7,5},{8,10},{9,11},{10,... | collective-permute-start | bytes 786440 | tf_op jit(solution)/shard_map/ppermute | solution.py:429
